TPU v7x, 32 devices: a whole 2x2x4 slice. The times are simulated.
32 devices in a mesh: region: 16 (over z, y, core), panel: 2 (over x).
Axes of the slice: x: 2, y: 2, z: 4, core: 2. Of those that a mesh axis runs over, the one named last changes fastest.
Arguments:
- multipliers: bfloat16 [16, 4096, 512], P('region', 'panel'), may hold values from -6 to 6
- flexibility: bfloat16 [16, 4096, 4096], P('region', 'panel'), as said below
- interface_sizes: int32 [16], P('region'), may hold values from 1024 to 4096, as said below
- send_rows: int32 [16, 2, 1536], replicated, may hold values from 0 to 4095, as said below
- recv_rows: int32 [16, 2, 1536], P('region'), may hold values from 0 to 4095, as said below
- recv_pos: int32 [16, 2, 1536], P('region'), may hold values from 0 to 1534
- recv_weight: float32 [16, 2, 1536], P('region'), may hold values from 0 to 1
Outputs:
- dual_image: float32 [16, 4096, 512], P('region', None, 'panel')
Inputs may be any that keep to these rules, and one draw needn't show every extreme that they name: `flexibility`: each region's matrix is symmetric. `interface_sizes`: A multiple of 128. `send_rows`: every entry of region r is below interface_sizes[r]; side 0 faces region r - 1 and side 1 region r + 1 around the loop; rows may repeat. `recv_rows`: every entry of region r is below interface_sizes[r]; rows may repeat.
All inputs are finite; a program needn't handle non-finite values.
Results may differ from a plain program's by a relative error of at most 0.0029.
Values may be sent and summed in bfloat16 or wider, within the bound.
No kernel may reach another device: no remote copies, remote signals or barrier semaphores. Data moves between devices by JAX's collectives and lax.ppermute only.
A program may use at most 128 MiB of HBM per device.

v0:
```python
import jax
import jax.numpy as jnp
from jax import lax
from jax.sharding import PartitionSpec as P


def shifted(value, axis, steps):
    count = lax.axis_size(axis)
    pairs = [(source, (source + steps) % count) for source in range(count)]
    return lax.ppermute(value, axis, pairs)


def interpolate(arrived, position, weight):
    first_rows = arrived[position].astype(jnp.float32)
    second_rows = arrived[position + 1].astype(jnp.float32)
    return (1.0 - weight)[:, None] * first_rows + weight[:, None] * second_rows


def on_device(
    multipliers, flexibility, interface_sizes, send_rows, recv_rows, recv_pos, recv_weight
):
    local_block = multipliers[0]
    flex_panel = flexibility[0]
    rows_here = local_block.shape[0]
    first_row = lax.axis_index("panel") * rows_here
    row_ids = first_row + jnp.arange(rows_here, dtype=jnp.int32)
    live_here = (row_ids < interface_sizes[0])[:, None]
    live_block = jnp.where(live_here, local_block, jnp.zeros((), local_block.dtype))
    image = jnp.dot(
        flex_panel,
        lax.all_gather(live_block, "panel", axis=0, tiled=True),
        preferred_element_type=jnp.float32,
    )
    settled = jnp.where(live_here, image, jnp.zeros((), image.dtype)).astype(jnp.bfloat16)
    columns_all = lax.all_to_all(settled, "panel", split_axis=1, concat_axis=0, tiled=True)
    region_index = lax.axis_index("region")
    regions = lax.axis_size("region")
    lower_region = (region_index + regions - 1) % regions
    upper_region = (region_index + 1) % regions
    lower_all = shifted(columns_all, "region", 1)
    upper_all = shifted(columns_all, "region", -1)
    from_lower = lower_all[send_rows[lower_region, 1]]
    from_upper = upper_all[send_rows[upper_region, 0]]
    jump_lower = interpolate(from_lower, recv_pos[0, 0], recv_weight[0, 0])
    jump_upper = interpolate(from_upper, recv_pos[0, 1], recv_weight[0, 1])
    jumps = jnp.concatenate([jump_lower, jump_upper], axis=0)
    targets = recv_rows[0].reshape(-1)
    result = columns_all.astype(jnp.float32).at[targets].add(-jumps)
    return result[None]


def solution(mesh):
    in_specs = (
        P("region", "panel", None),
        P("region", "panel", None),
        P("region"),
        P(),
        P("region", None, None),
        P("region", None, None),
        P("region", None, None),
    )
    out_specs = P("region", None, "panel")
    return jax.shard_map(
        on_device, mesh=mesh, in_specs=in_specs, out_specs=out_specs, check_vma=False
    )
```

profile of v0, /device:TPU:1, one launch (start us, length us, event | category | flops | bytes accessed | tf_op | source)
XLA Modules:
  0.0 225.4 jit_solution(8095538490072219212)
XLA Ops:
  6.5 0.0 all-gather.2.cloned.1.call-start
  7.2 2.8 %bitcast_select_fusion = bf16[2048,512]{1,0:T(8,128)(2,1)} fusion(bf16[1,2048,512]{2,1,0:T(8,128)(2,1)} %param.7, pred[2048]{0:T(1024)(128)(4,1)S(1)} %add_compare_fusion), kind=kLoop, calls=%fused_computation.14 | loop fusion | flops 1048576 | bytes 4196352 | tf_op jit(solution)/shard_map/jit(_where)/select_n | solution.py:28
  10.0 0.0 all-gather.2.cloned.1.call-update
  10.0 58.8 %all-gather.2.cloned.1.call-done = bf16[4096,512]{1,0:T(8,128)(2,1)} async-done(((bf16[2048,512]{1,0:T(8,128)(2,1)}), bf16[4096,512]{1,0:T(8,128)(2,1)}) %all-gather.2.cloned.1.call-update) | async-done | bytes 4194320 | tf_op jit(solution)/shard_map/all_gather | solution.py:31
  68.8 14.7 %select_convert_fusion = bf16[512,2048]{1,0:T(8,128)(2,1)} fusion(bf16[4096,512]{1,0:T(8,128)(2,1)} %all-gather.2.cloned.1.call-done, bf16[1,2048,4096]{2,1,0:T(8,128)(2,1)} %param.8, pred[2048]{0:T(1024)(128)(4,1)S(1)} %add_compare_fusion), kind=kOutput, calls=%fused_computation.9 | convolution fusion | flops 8592031744 | bytes 23070720 | tf_op jit(solution)/shard_map/dot_general | solution.py:29
  83.4 0.0 copy-start.4
  83.4 3.9 %all-to-all-start = ((bf16[2048,2,256]{0,2,1:T(8,128)(2,1)}), bf16[2048,2,256]{0,2,1:T(8,128)(2,1)S(1)}, u32[]{:S(2)}, u32[]{:S(2)}) async-start(bf16[2048,2,256]{0,2,1:T(8,128)(2,1)} %bitcast.42), calls=%async_computation | async-start | bytes 4194304 | tf_op jit(solution)/shard_map/all_to_all | solution.py:35
  87.4 0.8 fusion.7
  88.1 0.0 copy-done.4
  88.2 0.1 fusion.8
  88.3 23.1 %all-to-all-done = bf16[2048,2,256]{0,2,1:T(8,128)(2,1)S(1)} async-done(((bf16[2048,2,256]{0,2,1:T(8,128)(2,1)}), bf16[2048,2,256]{0,2,1:T(8,128)(2,1)S(1)}, u32[]{:S(2)}, u32[]{:S(2)}) %all-to-all-start) | async-done | bytes 2097184 | tf_op jit(solution)/shard_map/all_to_all | solution.py:35
  111.4 0.0 copy-start.3
  111.4 2.5 %copy.9 = bf16[2,2048,256]{2,1,0:T(8,128)(2,1)} copy(bf16[2,2048,256]{1,2,0:T(8,128)(2,1)S(1)} %bitcast.41) | data formatting | bytes 4194304 | tf_op jit(solution)/shard_map/all_to_all | solution.py:35
  113.9 2.8 %collective-permute-start = (bf16[4096,256]{1,0:T(8,128)(2,1)}, bf16[4096,256]{1,0:T(8,128)(2,1)}, u32[]{:S(2)}, u32[]{:S(2)}) collective-permute-start(bf16[4096,256]{1,0:T(8,128)(2,1)} %bitcast.6), channel_id=1, source_target_pairs={{0,2},{2,4},{4,6},{6,8},{8,10},{10,12},{12,14},{14,16},{16,18},{18... | collective-permute-start | bytes 6291464 | tf_op jit(solution)/shard_map/ppermute | solution.py:10
  116.7 0.0 collective-permute-start.1
  116.7 0.0 copy-done.3
  116.7 0.0 copy-done.2
  116.8 3.9 %bitcast_convert_fusion = f32[4096,256]{1,0:T(8,128)} fusion(bf16[2,2048,256]{2,1,0:T(8,128)(2,1)} %copy.9), kind=kLoop, calls=%fused_computation.45 | loop fusion | flops 1048576 | bytes 6291456 | tf_op jit(solution)/shard_map/convert_element_type | solution.py:48
  120.7 41.7 %collective-permute-done = bf16[4096,256]{1,0:T(8,128)(2,1)} collective-permute-done((bf16[4096,256]{1,0:T(8,128)(2,1)}, bf16[4096,256]{1,0:T(8,128)(2,1)}, u32[]{:S(2)}, u32[]{:S(2)}) %collective-permute-start) | collective-permute-done | bytes 2097184 | tf_op jit(solution)/shard_map/ppermute | solution.py:10
  162.4 5.5 %gather_fusion = bf16[1536,256]{1,0:T(8,128)(2,1)S(1)} fusion(bf16[4096,256]{1,0:T(8,128)(2,1)} %collective-permute-done, s32[2048]{0:T(1024)S(1)} %pad_clamp_fusion.5), kind=kCustom, calls=%fused_computation | custom fusion | bytes 1579008 | tf_op jit(solution)/shard_map/gather | solution.py:42
  168.0 5.4 %gather_fusion.1 = bf16[1536,256]{1,0:T(8,128)(2,1)} fusion(bf16[1536,256]{1,0:T(8,128)(2,1)S(1)} %gather_fusion, s32[2048]{0:T(1024)S(1)} %get-tuple-element.16), kind=kCustom, calls=%fused_computation.1 | custom fusion | bytes 1579008 | tf_op jit(solution)/shard_map/gather | solution.py:14
  173.3 5.4 %gather_fusion.2 = bf16[1536,256]{1,0:T(8,128)(2,1)} fusion(bf16[1536,256]{1,0:T(8,128)(2,1)S(1)} %gather_fusion, s32[2048]{0:T(1024)S(1)} %get-tuple-element.15), kind=kCustom, calls=%fused_computation.2 | custom fusion | bytes 1579008 | tf_op jit(solution)/shard_map/gather | solution.py:15
  178.7 0.0 collective-permute-done.1
  178.7 4.8 %gather_fusion.3 = bf16[1536,256]{1,0:T(8,128)(2,1)S(1)} fusion(bf16[4096,256]{1,0:T(8,128)(2,1)S(1)} %collective-permute-done.1, s32[2048]{0:T(1024)S(1)} %pad_clamp_fusion.2), kind=kCustom, calls=%fused_computation.3 | custom fusion | bytes 1579008 | tf_op jit(solution)/shard_map/gather | solution.py:43
  183.4 5.4 %gather_fusion.4 = bf16[1536,256]{1,0:T(8,128)(2,1)} fusion(bf16[1536,256]{1,0:T(8,128)(2,1)S(1)} %gather_fusion.3, s32[2048]{0:T(1024)S(1)} %get-tuple-element.14), kind=kCustom, calls=%fused_computation.4 | custom fusion | bytes 1579008 | tf_op jit(solution)/shard_map/gather | solution.py:14
  188.8 5.3 %gather_fusion.5 = bf16[1536,256]{1,0:T(8,128)(2,1)} fusion(bf16[1536,256]{1,0:T(8,128)(2,1)S(1)} %gather_fusion.3, s32[2048]{0:T(1024)S(1)} %get-tuple-element.13), kind=kCustom, calls=%fused_computation.5 | custom fusion | bytes 1579008 | tf_op jit(solution)/shard_map/gather | solution.py:15
  194.1 0.0 copy-start
  194.1 2.0 multiply_add_fusion.1
  196.1 0.0 copy-done
  196.1 0.0 copy-done.1
  196.1 0.5 multiply_add_fusion
  196.6 22.0 %scatter_custom_fusion = f32[4096,256]{1,0:T(8,128)} fusion(f32[4096,256]{1,0:T(8,128)} %bitcast_convert_fusion, s32[3072]{0:T(1024)S(1)} %bitcast.45, f32[1536,256]{1,0:T(8,128)S(1)} %multiply_add_fusion, f32[]{:T(128)} %constant.63, f32[1536,256]{1,0:T(8,128)S(1)} %multiply_add_fusion.1), kind=kCustom, calls=%fused_computation.11 | custom fusion | flops 2359296 | bytes 7340544 | tf_op jit(solution)/shard_map/scatter-add | solution.py:48
  (11 shorter events, 0.1 us)
Async XLA Ops:
  6.5 62.2 %all-gather.2.cloned.1.call-start = ((), (), s32[]{:S(2)}) async-start(), calls=%async_computation.1 | async-start | bytes 6291456 | tf_op jit(solution)/shard_map/all_gather | solution.py:31
  83.4 4.7 %copy-start.4 = (s32[1,2,1536]{2,1,0:T(2,128)S(1)}, s32[1,2,1536]{2,1,0:T(2,128)}, u32[]{:S(2)}) copy-start(s32[1,2,1536]{2,1,0:T(2,128)} %param.12) | copy-start | bytes 36868
  83.4 28.0 %all-to-all-start = ((bf16[2048,2,256]{0,2,1:T(8,128)(2,1)}), bf16[2048,2,256]{0,2,1:T(8,128)(2,1)S(1)}, u32[]{:S(2)}, u32[]{:S(2)}) async-start(bf16[2048,2,256]{0,2,1:T(8,128)(2,1)} %bitcast.42), calls=%async_computation | async-start | bytes 4194304 | tf_op jit(solution)/shard_map/all_to_all | solution.py:35
  111.4 5.3 %copy-start.3 = (s32[1,2,1536]{2,1,0:T(2,128)S(1)}, s32[1,2,1536]{2,1,0:T(2,128)}, u32[]{:S(2)}) copy-start(s32[1,2,1536]{2,1,0:T(2,128)} %param.11) | copy-start | bytes 36868
  111.4 5.3 %copy-start.2 = (f32[1,2,1536]{2,1,0:T(2,128)S(1)}, f32[1,2,1536]{2,1,0:T(2,128)}, u32[]{:S(2)}) copy-start(f32[1,2,1536]{2,1,0:T(2,128)} %param.13) | copy-start | bytes 36868
  113.9 48.5 %collective-permute-start = (bf16[4096,256]{1,0:T(8,128)(2,1)}, bf16[4096,256]{1,0:T(8,128)(2,1)}, u32[]{:S(2)}, u32[]{:S(2)}) collective-permute-start(bf16[4096,256]{1,0:T(8,128)(2,1)} %bitcast.6), channel_id=1, source_target_pairs={{0,2},{2,4},{4,6},{6,8},{8,10},{10,12},{12,14},{14,16},{16,18},{18... | collective-permute-start | bytes 6291464 | tf_op jit(solution)/shard_map/ppermute | solution.py:10
  116.7 62.0 %collective-permute-start.1 = (bf16[4096,256]{1,0:T(8,128)(2,1)}, bf16[4096,256]{1,0:T(8,128)(2,1)S(1)}, u32[]{:S(2)}, u32[]{:S(2)}) collective-permute-start(bf16[4096,256]{1,0:T(8,128)(2,1)} %bitcast.6), channel_id=1, source_target_pairs={{0,30},{2,0},{4,2},{6,4},{8,6},{10,8},{12,10},{14,12},{16,14},{18,... | collective-permute-start | bytes 6291464 | tf_op jit(solution)/shard_map/ppermute | solution.py:10
  194.1 2.0 copy-start
  194.1 2.0 copy-start.1
Sparse Core Ops, SparseCore 0:
  10.1 58.6 all-gather.1
where the time goes:
time: 226 us; the launch traced here: 225 us
  waiting for transfers between devices  124 us (55%)
  local copies, waits for them, and re-layouts  34.2 us (15%)
  other arithmetic  32 us (14%)
  matrix products  14.7 us (7%)
  between operations  14.2 us (6%)
  starting transfers between devices  6.68 us (3%)
    all_gather x1, waiting for transfers between devices, on_device(): lax.all_gather(live_block, 'panel', axis=0, tiled=True)  58.8 us
    ppermute x2, waiting for transfers between devices, shifted(): return lax.ppermute(value, axis, pairs)  41.7 us
    all_to_all x1, waiting for transfers between devices, on_device(): lax.all_to_all(settled, 'panel', split_axis=1, concat_axis=0, tiled=True)  23.1 us
    scatter-add x1, other arithmetic, on_device(): result = columns_all.astype(jnp.float32).at[targets].add(-jumps)  22 us
    dot_general x1, matrix products, on_device(): jnp.dot(flex_panel, lax.all_gather(live_block, 'panel', axis=0, tiled=Tru...  14.7 us
    gather x2, local copies, waits for them, and re-layouts, interpolate(): first_rows = arrived[position].astype(jnp.float32)  10.7 us
    gather x2, local copies, waits for them, and re-layouts, interpolate(): second_rows = arrived[position + 1].astype(jnp.float32)  10.7 us
    gather x1, local copies, waits for them, and re-layouts, on_device(): from_lower = lower_all[send_rows[lower_region, 1]]  5.51 us
  transfers between devices with their start and end apart: 4, of which 3 were waited for; matrix products, arithmetic and copies ran while one was open for 9% of the time, Pallas kernels for 0%

commit v1 on v0

v1 whole, which is shorter than its diff:
```python
import functools

import jax
import jax.numpy as jnp
from jax import lax
from jax.experimental import pallas as pl
from jax.experimental.pallas import tpu as pltpu
from jax.sharding import PartitionSpec as P

SMEM = pltpu.SMEM


def params():
    return pltpu.CompilerParams(vmem_limit_bytes=56 * 1024 * 1024)


def cost(flops, moved):
    return pl.CostEstimate(flops=flops, bytes_accessed=moved, transcendentals=0)


def tile_of(extent, most):
    tile = most
    while extent % tile:
        tile //= 2
    return tile


def local_kernel(where_ref, flex_ref, other_ref, own_ref, part_ref, near_ref):
    flex = flex_ref[...]
    part_ref[...] = jnp.dot(flex, other_ref[...], preferred_element_type=jnp.float32)
    near_ref[...] = jnp.dot(flex, own_ref[...], preferred_element_type=jnp.float32)


def local_products(where, flex, other, own):
    rows, width = other.shape
    tile = tile_of(rows, 256)
    whole = pl.BlockSpec((rows, width), lambda i, w: (0, 0))
    strip = pl.BlockSpec((tile, width), lambda i, w: (i, 0))
    shape = jax.ShapeDtypeStruct((rows, width), jnp.float32)
    return pl.pallas_call(
        local_kernel,
        out_shape=(shape, shape),
        grid_spec=pltpu.PrefetchScalarGridSpec(
            num_scalar_prefetch=1,
            grid=(rows // tile,),
            in_specs=[pl.BlockSpec((tile, rows), lambda i, w: (i, w[0])), whole, whole],
            out_specs=(strip, strip),
        ),
        compiler_params=params(),
        cost_estimate=cost(4 * rows * rows * width, 2 * rows * rows + 12 * rows * width),
        name="local_products",
    )(where, flex, other, own)


def mirror_kernel(where_ref, flex_ref, own_ref, far_ref):
    far_ref[...] = lax.dot_general(
        flex_ref[...], own_ref[...], (((0,), (0,)), ((), ())),
        preferred_element_type=jnp.float32,
    )


def mirror_product(where, flex, own):
    rows, width = own.shape
    tile = tile_of(rows, 256)
    steps = rows // tile
    return pl.pallas_call(
        mirror_kernel,
        out_shape=jax.ShapeDtypeStruct((rows, width), jnp.float32),
        grid_spec=pltpu.PrefetchScalarGridSpec(
            num_scalar_prefetch=1,
            grid=(steps,),
            in_specs=[
                pl.BlockSpec((rows, tile), lambda i, w: (0, w[1] * steps + i)),
                pl.BlockSpec((rows, width), lambda i, w: (0, 0)),
            ],
            out_specs=pl.BlockSpec((tile, width), lambda i, w: (i, 0)),
        ),
        compiler_params=params(),
        cost_estimate=cost(2 * rows * rows * width, 2 * rows * rows + 6 * rows * width),
        name="mirror_product",
    )(where, flex, own)


def cross_kernel(where_ref, flex_ref, came_ref, near_ref, out_ref):
    out_ref[...] = near_ref[...] + jnp.dot(
        flex_ref[...], came_ref[...], preferred_element_type=jnp.float32
    )


def cross_product(where, flex, came, near):
    rows, width = came.shape
    tile = tile_of(rows, 256)
    strip = pl.BlockSpec((tile, width), lambda i, w: (i, 0))
    return pl.pallas_call(
        cross_kernel,
        out_shape=jax.ShapeDtypeStruct((rows, width), jnp.float32),
        grid_spec=pltpu.PrefetchScalarGridSpec(
            num_scalar_prefetch=1,
            grid=(rows // tile,),
            in_specs=[
                pl.BlockSpec((tile, rows), lambda i, w: (i, w[1])),
                pl.BlockSpec((rows, width), lambda i, w: (0, 0)),
                strip,
            ],
            out_specs=strip,
        ),
        compiler_params=params(),
        cost_estimate=cost(2 * rows * rows * width, 2 * rows * rows + 10 * rows * width),
        name="cross_product",
    )(where, flex, came, near)


def gather_kernel(list_ref, settled_ref, out_ref, rows_ref):
    count = out_ref.shape[0]

    def step(block, carry):
        first = pl.multiple_of(block * 8, 8)
        for k in range(8):
            source = list_ref[first + k]
            rows_ref[pl.ds(first + k, 1), :] = settled_ref[pl.ds(source, 1), :]
        return carry

    lax.fori_loop(0, count // 8, step, 0, unroll=2)
    out_ref[...] = rows_ref[...].astype(out_ref.dtype)


def gather_rows(rows_list, settled):
    count = rows_list.shape[0]
    rows, width = settled.shape
    return pl.pallas_call(
        gather_kernel,
        out_shape=jax.ShapeDtypeStruct((count, width), jnp.bfloat16),
        in_specs=[pl.BlockSpec(memory_space=SMEM), pl.BlockSpec(memory_space=pltpu.VMEM)],
        out_specs=pl.BlockSpec(memory_space=pltpu.VMEM),
        scratch_shapes=[pltpu.VMEM((count, width), jnp.float32)],
        compiler_params=params(),
        cost_estimate=cost(0, 4 * rows * width + 2 * count * width),
        name="gather_rows",
    )(rows_list, settled)


def assemble_kernel(target_ref, pos_ref, weight_ref, base_ref, came_ref, out_ref, rows_ref):
    count = came_ref.shape[0]
    out_ref[...] = base_ref[...]
    rows_ref[...] = came_ref[...].astype(jnp.float32)

    def step(block, carry):
        for k in range(8):
            s = block * 8 + k
            at = pos_ref[s]
            second = weight_ref[s]
            first = 1.0 - second
            jump = first * rows_ref[pl.ds(at, 1), :] + second * rows_ref[pl.ds(at + 1, 1), :]
            row = target_ref[s]
            out_ref[pl.ds(row, 1), :] = out_ref[pl.ds(row, 1), :] - jump
        return carry

    lax.fori_loop(0, count // 8, step, 0)


def assemble(targets, positions, weights, base, came):
    count, width = came.shape
    smem = pl.BlockSpec(memory_space=SMEM)
    vmem = pl.BlockSpec(memory_space=pltpu.VMEM)
    return pl.pallas_call(
        assemble_kernel,
        out_shape=jax.ShapeDtypeStruct(base.shape, jnp.float32),
        in_specs=[smem, smem, smem, vmem, vmem],
        out_specs=vmem,
        scratch_shapes=[pltpu.VMEM((count, width), jnp.float32)],
        compiler_params=params(),
        cost_estimate=cost(0, 8 * base.size + 2 * came.size),
        name="assemble",
    )(targets, positions, weights, base, came)


def on_device(
    multipliers, flexibility, interface_sizes, send_rows, recv_rows, recv_pos, recv_weight
):
    block = multipliers[0]
    flex = flexibility[0]
    rows, cases = block.shape
    width = cases // 2
    me = lax.axis_index("panel")
    other = 1 - me
    region = lax.axis_index("region")
    regions = lax.axis_size("region")
    side = region % 2
    size = interface_sizes[0]
    swap = [(0, 1), (1, 0)]
    inner = [(r, r ^ 1) for r in range(regions)]
    outer = [(r, (r + (1 if r % 2 else -1)) % regions) for r in range(regions)]

    ids = jnp.arange(rows, dtype=jnp.int32)[:, None]
    live_here = me * rows + ids < size
    live_there = other * rows + ids < size
    live_block = jnp.where(live_here, block, jnp.zeros((), block.dtype))
    own = lax.dynamic_slice_in_dim(live_block, me * width, width, axis=1)
    others = lax.dynamic_slice_in_dim(live_block, other * width, width, axis=1)
    came = lax.ppermute(others, "panel", swap)

    where = jnp.stack([me, other]).astype(jnp.int32)
    part, near = local_products(where, flex, others, own)
    top = jnp.maximum(jnp.max(jnp.abs(part)), 1e-30)
    power = jnp.floor(jnp.log2(top)) - 13.0
    payload = jnp.concatenate(
        [
            (part * jnp.exp2(-power)).astype(jnp.float16),
            jnp.full((16, width), power, jnp.float16),
        ],
        axis=0,
    )
    payload = lax.ppermute(payload, "panel", swap)
    far = mirror_product(where, flex, own)
    image_here = cross_product(where, flex, came, near)

    came_part = payload[:rows].astype(jnp.float32)
    came_power = jnp.exp2(payload[rows, 0].astype(jnp.float32))
    image_there = far + came_part * came_power
    zero = jnp.zeros((), jnp.float32)
    here = jnp.where(live_here, image_here, zero)
    there = jnp.where(live_there, image_there, zero)
    first = jnp.where(me == 0, here, there)
    last = jnp.where(me == 0, there, here)
    settled = lax.reduce_precision(jnp.concatenate([first, last], axis=0), 8, 7)

    lists = send_rows[region]
    slow = gather_rows(lists[side], settled)
    slow = lax.ppermute(slow, "region", outer)
    fast = gather_rows(lists[1 - side], settled)
    fast = lax.ppermute(fast, "region", inner)
    up = 1 - side
    result = assemble(recv_rows[0, up], recv_pos[0, up], recv_weight[0, up], settled, fast)
    result = assemble(recv_rows[0, side], recv_pos[0, side], recv_weight[0, side], result, slow)
    return result[None]


def solution(mesh):
    assert mesh.shape["panel"] == 2 and mesh.shape["region"] % 2 == 0
    in_specs = (
        P("region", "panel", None),
        P("region", "panel", None),
        P("region"),
        P(),
        P("region", None, None),
        P("region", None, None),
        P("region", None, None),
    )
    out_specs = P("region", None, "panel")
    return jax.shard_map(
        on_device, mesh=mesh, in_specs=in_specs, out_specs=out_specs, check_vma=False
    )
```

time: 226 us -> 115 us (0.51)
  the two profiles are of different devices: /device:TPU:1 before, /device:TPU:0 now
where the time goes in v1:
time: 115 us; the launch traced here: 114 us
  Pallas kernels  77.2 us (67%)
  other arithmetic  10.6 us (9%)
  waiting for transfers between devices  9.04 us (8%)
  starting transfers between devices  7.96 us (7%)
  local copies, waits for them, and re-layouts  6.83 us (6%)
  between operations  2.22 us (2%)
    pallas_call x2, Pallas kernels, assemble(): pl.pallas_call(assemble_kernel, out_shape=jax.ShapeDtypeStruct(base.shape...  29.3 us
    pallas_call x2, Pallas kernels, gather_rows(): pl.pallas_call(gather_kernel, out_shape=jax.ShapeDtypeStruct((count, widt...  16.8 us
    pallas_call x1, Pallas kernels, local_products(): pl.pallas_call(local_kernel, out_shape=(shape, shape), grid_spec=pltpu.Pr...  11.4 us
    pallas_call x1, Pallas kernels, cross_product(): pl.pallas_call(cross_kernel, out_shape=jax.ShapeDtypeStruct((rows, width)...  9.92 us
    pallas_call x1, Pallas kernels, mirror_product(): pl.pallas_call(mirror_kernel, out_shape=jax.ShapeDtypeStruct((rows, width...  9.74 us
    ppermute x1, waiting for transfers between devices, on_device(): payload = lax.ppermute(payload, 'panel', swap)  9.03 us
    ppermute x1, starting transfers between devices, on_device(): slow = lax.ppermute(slow, 'region', outer)  4.92 us
    select_n x1, other arithmetic, on_device(): first = jnp.where(me == 0, here, there)  3.12 us
  transfers between devices with their start and end apart: 4, of which 1 were waited for; matrix products, arithmetic and copies ran while one was open for 6% of the time, Pallas kernels for 48%

profile of v1, /device:TPU:0, one launch (start us, length us, event | category | flops | bytes accessed | tf_op | source)
XLA Modules:
  0.0 113.9 jit_solution(14561570444062632511)
XLA Ops:
  0.7 1.8 %bitcast_select_fusion = bf16[2048,512]{1,0:T(8,128)(2,1)S(1)} fusion(bf16[1,2048,512]{2,1,0:T(8,128)(2,1)} %param.7, pred[2048]{0:T(1024)(128)(4,1)S(1)} %add_compare_fusion.1), kind=kLoop, calls=%fused_computation.1 | loop fusion | flops 1048576 | bytes 4196352 | tf_op jit(solution)/shard_map/jit(_where)/select_n | solution.py:197
  2.4 1.5 %constant_dynamic-slice_fusion = (bf16[2048,256]{1,0:T(8,128)(2,1)}, bf16[2048,256]{1,0:T(8,128)(2,1)}) fusion(bf16[2048,512]{1,0:T(8,128)(2,1)S(1)} %bitcast_select_fusion, s32[]{:T(128)S(6)} %select_n.63, s32[]{:T(128)S(6)} %select_n.62), kind=kLoop, calls=%fused_computation.17 | loop fusion | bytes 4194312 | tf_op jit(solution)/shard_map/dynamic_slice | solution.py:198
  3.9 3.0 %collective-permute-start = (bf16[2048,256]{1,0:T(8,128)(2,1)}, bf16[2048,256]{1,0:T(8,128)(2,1)}, u32[]{:S(2)}, u32[]{:S(2)}) collective-permute-start(bf16[2048,256]{1,0:T(8,128)(2,1)} %get-tuple-element.20.other_ref), channel_id=1, source_target_pairs={{0,1},{1,0},{2,3},{3,2},{4,5},{5,4},{6,7},{7,6},{8,9},{9,8},{10,11... | collective-permute-start | bytes 3145736 | tf_op jit(solution)/shard_map/ppermute | solution.py:200
  6.9 0.6 pad_add_fusion.where_ref
  7.5 11.4 %local_products.1 = (f32[2048,256]{1,0:T(8,128)}, f32[2048,256]{1,0:T(8,128)}) custom-call(s32[2]{0:T(128)} %pad_add_fusion.where_ref, bf16[2048,4096]{1,0:T(8,128)(2,1)} %bitcast.10, bf16[2048,256]{1,0:T(8,128)(2,1)} %get-tuple-element.20.other_ref, bf16[2048,256]{1,0:T(8,128)(2,1)} %get-tuple-element.19.own_ref), custom_call_target="tpu_custom_call" | custom-call | flops 4294967296 | bytes 14680064 | tf_op jit(solution)/shard_map/local_products/pallas_call | solution.py:40
  19.0 2.5 %abs_reduce_fusion = f32[]{:T(128)} fusion(f32[2048,256]{1,0:T(8,128)} %get-tuple-element.8), kind=kLoop, calls=%fused_computation.4 | loop fusion | flops 1048575 | bytes 2097156 | tf_op jit(solution)/shard_map/reduce_max | solution.py:204
  22.2 0.0 copy-done
  22.2 0.3 multiply_convert_fusion
  22.4 0.2 concatenate.6
  22.7 0.1 collective-permute-start.1
  22.8 1.4 %dynamic-slice_reduce_fusion = (s32[1536]{0:T(1024)}, s32[1536]{0:T(1024)}) fusion(s32[16,2,1536]{2,1,0:T(2,128)} %param.10, s32[]{:T(128)S(6)} %select_n.69, s32[]{:T(128)S(6)} %select_n.71, s32[]{:T(128)S(6)} %select_n.70), kind=kLoop, calls=%fused_computation.9 | loop fusion | bytes 24588 | tf_op jit(solution)/shard_map/dynamic_slice | solution.py:228
  24.2 9.7 %mirror_product.1 = f32[2048,256]{1,0:T(8,128)} custom-call(s32[2]{0:T(128)} %pad_add_fusion.where_ref, bf16[2048,4096]{1,0:T(8,128)(2,1)} %bitcast.11, bf16[2048,256]{1,0:T(8,128)(2,1)} %get-tuple-element.19.own_ref), custom_call_target="tpu_custom_call" | custom-call | flops 2147483648 | bytes 11534336 | tf_op jit(solution)/shard_map/mirror_product/pallas_call | solution.py:66
  34.0 0.0 collective-permute-done.came_ref
  34.0 9.9 %cross_product.1 = f32[2048,256]{1,0:T(8,128)} custom-call(s32[2]{0:T(128)} %pad_add_fusion.where_ref, bf16[2048,4096]{1,0:T(8,128)(2,1)} %bitcast.12, bf16[2048,256]{1,0:T(8,128)(2,1)} %collective-permute-done.came_ref, f32[2048,256]{1,0:T(8,128)} %get-tuple-element.7.near_ref), custom_call_target="tpu_custom_call" | custom-call | flops 2147483648 | bytes 13631488 | tf_op jit(solution)/shard_map/cross_product/pallas_call | solution.py:94
  43.9 9.0 %collective-permute-done.1 = f16[2064,256]{1,0:T(8,128)(2,1)S(1)} collective-permute-done((f16[2064,256]{1,0:T(8,128)(2,1)S(1)}, f16[2064,256]{1,0:T(8,128)(2,1)S(1)}, u32[]{:S(2)}, u32[]{:S(2)}) %collective-permute-start.1) | collective-permute-done | bytes 1056800 | tf_op jit(solution)/shard_map/ppermute | solution.py:213
  52.9 0.6 slice.9
  54.2 0.0 copy-done.1
  54.3 3.1 %select_select_fusion.1 = (f32[2048,256]{1,0:T(8,128)S(1)}, f32[2048,256]{1,0:T(8,128)S(1)}) fusion(f32[2048,256]{1,0:T(8,128)} %cross_product.1, f32[2048,256]{1,0:T(8,128)S(1)} %copy-done.1, f32[]{:T(128)} %bitcast.5, pred[2048]{0:T(1024)(128)(4,1)S(1)} %add_compare_fusion, pred[2048]{0:T(1024)(128)(4,1)S(1)} %add_compare_fusion.1, pred[]{:T(512)S(6)} %eq.6, ...), kind=kLoop, calls=%fused_computation.6 | loop fusion | flops 3670016 | bytes 9441285 | tf_op jit(solution)/shard_map/jit(_where)/select_n | solution.py:223
  57.4 2.3 %maximum_reduce-precision_fusion.settled_ref.base_ref = f32[4096,256]{1,0:T(8,128)} fusion(f32[2048,256]{1,0:T(8,128)S(1)} %get-tuple-element.18, f32[2048,256]{1,0:T(8,128)S(1)} %get-tuple-element.17), kind=kLoop, calls=%fused_computation | loop fusion | flops 2097152 | bytes 8388608 | tf_op jit(solution)/shard_map/reduce_precision | solution.py:225
  59.7 8.4 %gather_rows.2 = bf16[1536,256]{1,0:T(8,128)(2,1)} custom-call(s32[1536]{0:T(1024)} %get-tuple-element.10.list_ref, f32[4096,256]{1,0:T(8,128)} %maximum_reduce-precision_fusion.settled_ref.base_ref), custom_call_target="tpu_custom_call" | custom-call | bytes 4980736 | tf_op jit(solution)/shard_map/gather_rows/pallas_call | solution.py:130
  68.1 0.0 collective-permute-start.2
  68.1 0.0 copy-start.5
  68.1 8.4 %gather_rows.3 = bf16[1536,256]{1,0:T(8,128)(2,1)} custom-call(s32[1536]{0:T(1024)} %get-tuple-element.9.list_ref, f32[4096,256]{1,0:T(8,128)} %maximum_reduce-precision_fusion.settled_ref.base_ref), custom_call_target="tpu_custom_call" | custom-call | bytes 4980736 | tf_op jit(solution)/shard_map/gather_rows/pallas_call | solution.py:130
  76.5 4.9 %collective-permute-start.3 = (bf16[1536,256]{1,0:T(8,128)(2,1)}, bf16[1536,256]{1,0:T(8,128)(2,1)S(1)}, u32[]{:S(2)}, u32[]{:S(2)}) collective-permute-start(bf16[1536,256]{1,0:T(8,128)(2,1)} %gather_rows.3), channel_id=1, source_target_pairs={{0,30},{2,4},{4,2},{6,8},{8,6},{10,12},{12,10},{14,16},{16,14},{18... | collective-permute-start | bytes 2359304 | tf_op jit(solution)/shard_map/ppermute | solution.py:229
  81.4 0.6 dynamic-slice_reduce_fusion.2
  82.1 0.7 dynamic-slice_reduce_fusion.3
  82.8 0.0 collective-permute-done.2.came_ref
  82.8 0.9 copy-done.3
  83.7 14.6 %assemble.2.base_ref = f32[4096,256]{1,0:T(8,128)} custom-call(s32[1536]{0:T(1024)} %get-tuple-element.22.target_ref, s32[1536]{0:T(1024)} %get-tuple-element.13.pos_ref, f32[1536]{0:T(1024)} %get-tuple-element.11.weight_ref, f32[4096,256]{1,0:T(8,128)} %maximum_reduce-precision_fusion.settled_ref.base_ref, bf16[1536,256]{1,0:T(8,128)(2,1)} %copy-done.3), custom_call_target="tpu_custom_call" | custom-call | bytes 9175040 | tf_op jit(solution)/shard_map/assemble/pallas_call | solution.py:165
  98.3 0.0 collective-permute-done.3.came_ref
  98.3 0.9 copy-done.2
  99.2 14.7 %assemble.3 = f32[4096,256]{1,0:T(8,128)} custom-call(s32[1536]{0:T(1024)} %get-tuple-element.21.target_ref, s32[1536]{0:T(1024)} %get-tuple-element.14.pos_ref, f32[1536]{0:T(1024)} %get-tuple-element.12.weight_ref, f32[4096,256]{1,0:T(8,128)} %assemble.2.base_ref, bf16[1536,256]{1,0:T(8,128)(2,1)} %copy-done.2), custom_call_target="tpu_custom_call" | custom-call | bytes 9175040 | tf_op jit(solution)/shard_map/assemble/pallas_call | solution.py:165
  (11 shorter events, 0.0 us)
Async XLA Ops:
  3.9 30.0 %collective-permute-start = (bf16[2048,256]{1,0:T(8,128)(2,1)}, bf16[2048,256]{1,0:T(8,128)(2,1)}, u32[]{:S(2)}, u32[]{:S(2)}) collective-permute-start(bf16[2048,256]{1,0:T(8,128)(2,1)} %get-tuple-element.20.other_ref), channel_id=1, source_target_pairs={{0,1},{1,0},{2,3},{3,2},{4,5},{5,4},{6,7},{7,6},{8,9},{9,8},{10,11... | collective-permute-start | bytes 3145736 | tf_op jit(solution)/shard_map/ppermute | solution.py:200
  19.0 3.2 %copy-start = (f32[2048,256]{1,0:T(8,128)S(1)}, f32[2048,256]{1,0:T(8,128)}, u32[]{:S(2)}) copy-start(f32[2048,256]{1,0:T(8,128)} %get-tuple-element.8) | copy-start | bytes 6291460
  22.7 30.2 %collective-permute-start.1 = (f16[2064,256]{1,0:T(8,128)(2,1)S(1)}, f16[2064,256]{1,0:T(8,128)(2,1)S(1)}, u32[]{:S(2)}, u32[]{:S(2)}) collective-permute-start(f16[2064,256]{1,0:T(8,128)(2,1)S(1)} %concatenate.6), channel_id=1, source_target_pairs={{0,1},{1,0},{2,3},{3,2},{4,5},{5,4},{6,7},{7,6},{8,9},{9,8},{10,11... | collective-permute-start | bytes 3170312 | tf_op jit(solution)/shard_map/ppermute | solution.py:213
  34.0 20.3 %copy-start.1 = (f32[2048,256]{1,0:T(8,128)S(1)}, f32[2048,256]{1,0:T(8,128)}, u32[]{:S(2)}) copy-start(f32[2048,256]{1,0:T(8,128)} %mirror_product.1) | copy-start | bytes 6291460
  68.1 14.7 %collective-permute-start.2 = (bf16[1536,256]{1,0:T(8,128)(2,1)}, bf16[1536,256]{1,0:T(8,128)(2,1)S(1)}, u32[]{:S(2)}, u32[]{:S(2)}) collective-permute-start(bf16[1536,256]{1,0:T(8,128)(2,1)} %gather_rows.2), channel_id=1, source_target_pairs={{0,2},{2,0},{4,6},{6,4},{8,10},{10,8},{12,14},{14,12},{16,18},{18,... | collective-permute-start | bytes 2359304 | tf_op jit(solution)/shard_map/ppermute | solution.py:231
  68.1 13.4 %copy-start.6 = (f32[1,2,1536]{2,1,0:T(2,128)S(1)}, f32[1,2,1536]{2,1,0:T(2,128)}, u32[]{:S(2)}) copy-start(f32[1,2,1536]{2,1,0:T(2,128)} %param.13) | copy-start | bytes 36868
  68.1 14.0 %copy-start.4 = (s32[1,2,1536]{2,1,0:T(2,128)S(1)}, s32[1,2,1536]{2,1,0:T(2,128)}, u32[]{:S(2)}) copy-start(s32[1,2,1536]{2,1,0:T(2,128)} %param.12) | copy-start | bytes 36868
  68.1 14.0 %copy-start.5 = (s32[1,2,1536]{2,1,0:T(2,128)S(1)}, s32[1,2,1536]{2,1,0:T(2,128)}, u32[]{:S(2)}) copy-start(s32[1,2,1536]{2,1,0:T(2,128)} %param.11) | copy-start | bytes 36868
  76.5 21.8 %collective-permute-start.3 = (bf16[1536,256]{1,0:T(8,128)(2,1)}, bf16[1536,256]{1,0:T(8,128)(2,1)S(1)}, u32[]{:S(2)}, u32[]{:S(2)}) collective-permute-start(bf16[1536,256]{1,0:T(8,128)(2,1)} %gather_rows.3), channel_id=1, source_target_pairs={{0,30},{2,4},{4,2},{6,8},{8,6},{10,12},{12,10},{14,16},{16,14},{18... | collective-permute-start | bytes 2359304 | tf_op jit(solution)/shard_map/ppermute | solution.py:229
  82.8 0.9 copy-start.3
  98.3 0.9 copy-start.2

commit v2 on v0

v2 whole, which is shorter than its diff:
```python
import jax
import jax.numpy as jnp
from jax import lax
from jax.experimental import pallas as pl
from jax.experimental.pallas import tpu as pltpu
from jax.sharding import PartitionSpec as P

SMEM = pl.BlockSpec(memory_space=pltpu.SMEM)
VMEM = pl.BlockSpec(memory_space=pltpu.VMEM)
ANY = pl.BlockSpec(memory_space=pl.ANY)
HBM = pl.BlockSpec(memory_space=pltpu.HBM)
LANES = 128
F32 = jnp.float32
BF16 = jnp.bfloat16


def params(mebibytes):
    return pltpu.CompilerParams(vmem_limit_bytes=mebibytes * 1024 * 1024)


def cost(flops, moved):
    return pl.CostEstimate(flops=flops, bytes_accessed=moved, transcendentals=0)


def tile_of(extent, most):
    tile = most
    while extent % tile:
        tile //= 2
    return tile


def strips_of(flex_ref, block, buffer_ref, sems):
    rows = buffer_ref.shape[0]
    count = sems.shape[0]
    tile = rows // count
    start = pl.multiple_of(block * rows, rows)
    copies = []
    for i in range(count):
        span = pl.ds(i * tile, tile)
        copy = pltpu.make_async_copy(
            flex_ref.at[span, pl.ds(start, rows)], buffer_ref.at[span, :], sems.at[i]
        )
        copy.start()
        copies.append(copy)
    return copies, tile


def store_chunks(refs, span, value):
    for c, ref in enumerate(refs):
        ref[span, :] = value[:, c * LANES : (c + 1) * LANES]


def masked(ref, live):
    value = ref[...]
    ids = lax.broadcasted_iota(jnp.int32, value.shape, 0)
    return jnp.where(ids < live, value, jnp.zeros_like(value))


def part_kernel(where_ref, flex_ref, other_ref, *rest):
    outs, buffer_ref, sems = rest[:-2], rest[-2], rest[-1]
    copies, tile = strips_of(flex_ref, where_ref[0], buffer_ref, sems)
    right = masked(other_ref, where_ref[2])
    rows = buffer_ref.shape[0]
    most = jnp.zeros((8, right.shape[1]), F32)
    for i, copy in enumerate(copies):
        copy.wait()
        span = pl.ds(i * tile, tile)
        part = jnp.dot(buffer_ref[span, :], right, preferred_element_type=F32)
        store_chunks(outs, span, part)
        most = jnp.maximum(most, jnp.max(jnp.abs(part).reshape(-1, 8, part.shape[1]), axis=0))
    top = jnp.maximum(jnp.max(most, keepdims=True), 1e-30)
    power = jnp.floor(jnp.log2(top)) - 13.0
    scale = jnp.exp2(-power)
    for ref in outs:
        ref[pl.ds(0, rows), :] = ref[pl.ds(0, rows), :] * scale
        ref[pl.ds(rows, 16), :] = jnp.broadcast_to(power, (16, LANES))


def cross_kernel(where_ref, flex_ref, came_ref, *rest):
    count = (len(rest) - 2) // 2
    nears, outs, buffer_ref, sems = rest[:count], rest[count:-2], rest[-2], rest[-1]
    copies, tile = strips_of(flex_ref, where_ref[1], buffer_ref, sems)
    right = masked(came_ref, where_ref[3])
    for i, copy in enumerate(copies):
        copy.wait()
        span = pl.ds(i * tile, tile)
        image = jnp.dot(buffer_ref[span, :], right, preferred_element_type=F32)
        image = image + jnp.concatenate([ref[span, :] for ref in nears], axis=1)
        ids = i * tile + lax.broadcasted_iota(jnp.int32, image.shape, 0)
        image = jnp.where(ids < where_ref[2], image, jnp.zeros_like(image))
        store_chunks(outs, span, image.astype(BF16).astype(F32))


def product(kernel, name, out_shapes, where, flex, *rights):
    rows = flex.shape[0]
    width = rights[0].shape[1]
    strips = rows // tile_of(rows, 512)
    return pl.pallas_call(
        kernel,
        out_shape=tuple(jax.ShapeDtypeStruct(shape, F32) for shape in out_shapes),
        in_specs=[SMEM, HBM] + [VMEM] * len(rights),
        out_specs=tuple(VMEM for _ in out_shapes),
        scratch_shapes=[
            pltpu.VMEM((rows, rows), BF16),
            pltpu.SemaphoreType.DMA((strips,)),
        ],
        compiler_params=params(50),
        cost_estimate=cost(2 * rows * rows * width, 2 * rows * rows + 6 * rows * width),
        name=name,
    )(where, flex, *rights)


def own_kernel(where_ref, flex_ref, own_ref, *outs):
    tile = flex_ref.shape[0]
    rows = own_ref.shape[0]
    chunks = len(outs) // 2
    step = pl.program_id(0)
    right = masked(own_ref, where_ref[2])
    columns = [pl.ds(pl.multiple_of(where_ref[b] * rows, rows), rows) for b in range(2)]
    near = jnp.dot(flex_ref[:, columns[0]], right, preferred_element_type=F32)
    store_chunks(outs[:chunks], slice(None), near)
    span = pl.ds(pl.multiple_of(step * tile, tile), tile)
    mine = own_ref[span, :]
    ids = step * tile + lax.broadcasted_iota(jnp.int32, mine.shape, 0)
    mine = jnp.where(ids < where_ref[2], mine, jnp.zeros_like(mine))
    far = lax.dot_general(
        flex_ref[:, columns[1]], mine, (((0,), (0,)), ((), ())), preferred_element_type=F32
    )
    for c, ref in enumerate(outs[chunks:]):
        piece = far[:, c * LANES : (c + 1) * LANES]

        @pl.when(step == 0)
        def _():
            ref[...] = piece

        @pl.when(step > 0)
        def _():
            ref[...] = ref[...] + piece


def own_products(where, flex, own):
    rows, width = own.shape
    chunks = width // LANES
    tile = tile_of(rows, 512)
    shape = jax.ShapeDtypeStruct((rows, LANES), F32)
    outs = pl.pallas_call(
        own_kernel,
        out_shape=(shape,) * (2 * chunks),
        grid_spec=pltpu.PrefetchScalarGridSpec(
            num_scalar_prefetch=1,
            grid=(rows // tile,),
            in_specs=[
                pl.BlockSpec((tile, 2 * rows), lambda i, w: (i, 0)),
                pl.BlockSpec((rows, width), lambda i, w: (0, 0)),
            ],
            out_specs=(pl.BlockSpec((tile, LANES), lambda i, w: (i, 0)),) * chunks
            + (pl.BlockSpec((rows, LANES), lambda i, w: (0, 0)),) * chunks,
        ),
        compiler_params=params(50),
        cost_estimate=cost(4 * rows * rows * width, 4 * rows * rows + 10 * rows * width),
        name="own_products",
    )(where, flex, own)
    return outs[:chunks], outs[chunks:]


def pick_rows(list_ref, settled_ref, out_ref, rows_ref):
    count = out_ref.shape[0]
    group = tile_of(count, 32)

    def step(block, carry):
        first = pl.multiple_of(block * group, group)
        for k in range(group):
            source = list_ref[first + k]
            rows_ref[pl.ds(first + k, 1), :] = settled_ref[pl.ds(source, 1), :]
        return carry

    lax.fori_loop(0, count // group, step, 0)
    out_ref[...] = rows_ref[...].astype(out_ref.dtype)


def settle_kernel(list_ref, live_ref, here_ref, far_ref, came_ref, settled_ref, out_ref, rows_ref):
    rows = far_ref.shape[0]
    settled_ref[pl.ds(0, rows), :] = here_ref[...]
    grown = jnp.exp2(came_ref[pl.ds(rows, 1), :])
    there = far_ref[...] + came_ref[pl.ds(0, rows), :] * grown
    ids = lax.broadcasted_iota(jnp.int32, there.shape, 0)
    there = jnp.where(ids < live_ref[0], there, jnp.zeros_like(there))
    settled_ref[pl.ds(rows, rows), :] = there.astype(BF16).astype(F32)
    pick_rows(list_ref, settled_ref, out_ref, rows_ref)


def settle(rows_list, live, here, far, came):
    count = rows_list.shape[0]
    rows, lanes = far.shape
    return pl.pallas_call(
        settle_kernel,
        out_shape=(
            jax.ShapeDtypeStruct((2 * rows, lanes), F32),
            jax.ShapeDtypeStruct((count, lanes), BF16),
        ),
        in_specs=[SMEM, SMEM, VMEM, VMEM, VMEM],
        out_specs=(VMEM, VMEM),
        scratch_shapes=[pltpu.VMEM((count, lanes), F32)],
        compiler_params=params(20),
        cost_estimate=cost(0, 20 * rows * lanes + 2 * count * lanes),
        name="settle",
    )(rows_list, live, here, far, came)


def gather_rows(rows_list, settled):
    count = rows_list.shape[0]
    lanes = settled.shape[1]
    return pl.pallas_call(
        pick_rows,
        out_shape=jax.ShapeDtypeStruct((count, lanes), BF16),
        in_specs=[SMEM, VMEM],
        out_specs=VMEM,
        scratch_shapes=[pltpu.VMEM((count, lanes), F32)],
        compiler_params=params(8),
        cost_estimate=cost(0, 4 * settled.size + 2 * count * lanes),
        name="gather_rows",
    )(rows_list, settled)


def assemble_kernel(
    chunk, blocks_ref, targets_ref, places_ref, weights_ref, settled_ref, fast_ref, slow_ref, *rest
):
    out_ref, rows_refs, sums, sems = rest[-8], rest[-7:-5], rest[-5:-1], rest[-1]
    rows_refs[0][...] = fast_ref[...].astype(F32)
    rows_refs[1][...] = slow_ref[...].astype(F32)
    for ref in sums:
        ref[...] = jnp.zeros_like(ref)
    count = fast_ref.shape[0]
    group = tile_of(count, 32)

    def step(block, carry):
        start = pl.multiple_of(block * group, group)
        for k in range(group):
            for j in range(2):
                s = j * count + start + k
                row = targets_ref[s]
                at = places_ref[s]
                weight = weights_ref[pl.ds(s, 1), :]
                first = rows_refs[j][pl.ds(at, 1), :]
                second = rows_refs[j][pl.ds(at + 1, 1), :]
                jump = (1.0 - weight) * first + weight * second
                total = sums[(k % 2) * 2 + j]
                total[pl.ds(row, 1), :] = total[pl.ds(row, 1), :] + jump
        return carry

    lax.fori_loop(0, count // group, step, 0)
    rows = settled_ref.shape[0]
    piece = rows // 4
    copies = []
    for q in range(4):
        span = pl.ds(q * piece, piece)
        sums[0][span, :] = settled_ref[span, :] - (
            (sums[0][span, :] + sums[1][span, :]) + (sums[2][span, :] + sums[3][span, :])
        )
        target = pl.multiple_of(blocks_ref[q // 2] * (rows // 2) + (q % 2) * piece, piece)
        copy = pltpu.make_async_copy(
            sums[0].at[span, :],
            out_ref.at[pl.ds(target, piece), pl.ds(chunk * LANES, LANES)],
            sems.at[q],
        )
        copy.start()
        copies.append(copy)
    for copy in copies:
        copy.wait()


def assemble(chunk, width, blocks, targets, places, weights, settled, fast, slow, before):
    rows = settled.shape[0]
    count = fast.shape[0]
    more = [] if before is None else [before]
    return pl.pallas_call(
        lambda *refs: assemble_kernel(chunk, *refs),
        out_shape=jax.ShapeDtypeStruct((rows, width), F32),
        in_specs=[SMEM, SMEM, SMEM, VMEM, VMEM, VMEM, VMEM] + [ANY] * len(more),
        out_specs=ANY,
        scratch_shapes=[pltpu.VMEM((count, LANES), F32)] * 2
        + [pltpu.VMEM((rows, LANES), F32)] * 4
        + [pltpu.SemaphoreType.DMA((4,))],
        input_output_aliases={7: 0} if more else {},
        compiler_params=params(20),
        cost_estimate=cost(0, 8 * settled.size + 4 * fast.size),
        name="assemble",
    )(blocks, targets, places, weights, settled, fast, slow, *more)


def after(value, *earlier):
    return lax.optimization_barrier((value, *earlier))[0]


def on_device(
    multipliers, flexibility, interface_sizes, send_rows, recv_rows, recv_pos, recv_weight
):
    block = multipliers[0]
    flex = flexibility[0]
    rows, cases = block.shape
    width = cases // 2
    chunks = width // LANES
    me = lax.axis_index("panel")
    other = 1 - me
    region = lax.axis_index("region")
    regions = lax.axis_size("region")
    side = region % 2
    size = interface_sizes[0]
    swap = [(0, 1), (1, 0)]
    inner = [(r, r ^ 1) for r in range(regions)]
    outer = [(r, (r + (1 if r % 2 else -1)) % regions) for r in range(regions)]

    live_here = size - me * rows
    live_there = size - other * rows
    where = jnp.stack([me, other, live_here, live_there]).astype(jnp.int32)
    others = lax.dynamic_slice_in_dim(block, other * width, width, axis=1)
    came = lax.ppermute(others, "panel", swap)
    strip = (rows, LANES)

    def local_order(index):
        return (index + me * rows) % (2 * rows)

    lists = local_order(send_rows[region])
    slow_list, fast_list = lists[side], lists[1 - side]

    def ordered(table):
        return jnp.where(side == 0, table[::-1], table).reshape(-1)

    targets = ordered(local_order(recv_rows[0]))
    places = ordered(recv_pos[0])
    weights = jnp.broadcast_to(ordered(recv_weight[0])[:, None], (targets.shape[0], LANES))
    blocks = where[:2]
    live = live_there[None]

    parts = product(
        part_kernel, "part_product", [(rows + 16, LANES)] * chunks, where, flex, others
    )
    payloads = []
    order = others
    for c in range(chunks):
        order = after(parts[c], order).astype(jnp.float16)
        payloads.append(lax.ppermute(order, "panel", swap))
    own = lax.dynamic_slice_in_dim(after(block, order), me * width, width, axis=1)
    own, targets, places, weights, slow_list, fast_list = lax.optimization_barrier(
        (own, targets, places, weights, slow_list, fast_list)
    )
    nears, fars = own_products(where, flex, own)
    heres = product(
        cross_kernel, "cross_product", [strip] * chunks, where, flex, came, *nears
    )

    settled, slow, fast = [], [], []
    last = heres[0]
    for c in range(chunks):
        arrived = after(payloads[c], last).astype(F32)
        whole, sent = settle(slow_list, live, heres[c], fars[c], arrived)
        settled.append(whole)
        slow.append(lax.ppermute(sent, "region", outer))
        last = gather_rows(after(fast_list, sent), whole)
        fast.append(lax.ppermute(last, "region", inner))
    targets = after(targets, last)
    result = None
    for c in range(chunks):
        result = assemble(
            c, width, blocks, targets, places, weights, settled[c], fast[c], slow[c], result
        )
    return result[None]


def solution(mesh):
    assert mesh.shape["panel"] == 2 and mesh.shape["region"] % 2 == 0
    in_specs = (
        P("region", "panel", None),
        P("region", "panel", None),
        P("region"),
        P(),
        P("region", None, None),
        P("region", None, None),
        P("region", None, None),
    )
    out_specs = P("region", None, "panel")
    return jax.shard_map(
        on_device, mesh=mesh, in_specs=in_specs, out_specs=out_specs, check_vma=False
    )
```

time: 226 us -> 76.9 us (0.34)
  the two profiles are of different devices: /device:TPU:1 before, /device:TPU:0 now
where the time goes in v2:
time: 76.9 us; the launch traced here: 76.6 us
  Pallas kernels  50.7 us (66%)
  starting transfers between devices  13.3 us (17%)
  local copies, waits for them, and re-layouts  6.14 us (8%)
  other arithmetic  4.91 us (6%)
  between operations  1.07 us (1%)
    pallas_call x2, Pallas kernels, product(): pl.pallas_call(kernel, out_shape=tuple((jax.ShapeDtypeStruct(shape, F32)...  15.8 us
    pallas_call x2, Pallas kernels, assemble(): pl.pallas_call(lambda *refs: assemble_kernel(chunk, *refs), out_shape=jax...  15.1 us
    pallas_call x1, Pallas kernels, own_products(): pl.pallas_call(own_kernel, out_shape=(shape,) * (2 * chunks), grid_spec=p...  10.8 us
    ppermute x2, starting transfers between devices, on_device(): slow.append(lax.ppermute(sent, 'region', outer))  8.07 us
    pallas_call x2, Pallas kernels, settle(): pl.pallas_call(settle_kernel, out_shape=(jax.ShapeDtypeStruct((2 * rows,...  4.77 us
    pallas_call x2, Pallas kernels, gather_rows(): pl.pallas_call(pick_rows, out_shape=jax.ShapeDtypeStruct((count, lanes),...  4.18 us
    unnamed x14, local copies, waits for them, and re-layouts  3.55 us
    ppermute x1, starting transfers between devices, on_device(): came = lax.ppermute(others, 'panel', swap)  3.03 us
  transfers between devices with their start and end apart: 7, of which 1 were waited for; matrix products, arithmetic and copies ran while one was open for 10% of the time, Pallas kernels for 56%

profile of v2, /device:TPU:0, one launch (start us, length us, event | category | flops | bytes accessed | tf_op | source)
XLA Modules:
  0.0 76.6 jit_solution(4598204248199308120)
XLA Ops:
  0.0 1.6 %copy-done = bf16[1,2048,512]{2,1,0:T(8,128)(2,1)S(1)} copy-done((bf16[1,2048,512]{2,1,0:T(8,128)(2,1)S(1)}, bf16[1,2048,512]{2,1,0:T(8,128)(2,1)}, u32[]{:S(2)}) %copy-start) | copy-done | bytes 2097176
  1.6 0.1 dynamic-slice_bitcast_fusion.other_ref
  1.7 3.0 %collective-permute-start = (bf16[2048,256]{1,0:T(8,128)(2,1)S(1)}, bf16[2048,256]{1,0:T(8,128)(2,1)}, u32[]{:S(2)}, u32[]{:S(2)}) collective-permute-start(bf16[2048,256]{1,0:T(8,128)(2,1)S(1)} %dynamic-slice_bitcast_fusion.other_ref), channel_id=1, source_target_pairs={{0,1},{1,0},{2,3},{3,2},{4,5},{5,4},{6,7},{7,6},{8,9},{9,8},{10,11... | collective-permute-start | bytes 3145736 | tf_op jit(solution)/shard_map/ppermute | solution.py:317
  5.3 0.1 pad_add_fusion.1.where_ref
  5.4 7.4 %part_product.1 = (f32[2064,128]{1,0:T(8,128)S(1)}, f32[2064,128]{1,0:T(8,128)S(1)}) custom-call(s32[4]{0:T(128)S(1)} %pad_add_fusion.1.where_ref, bf16[2048,4096]{1,0:T(8,128)(2,1)} %bitcast.21, bf16[2048,256]{1,0:T(8,128)(2,1)S(1)} %dynamic-slice_bitcast_fusion.other_ref), custom_call_target="tpu_custom_call" | custom-call | flops 2147483648 | bytes 11534336 | tf_op jit(solution)/shard_map/part_product/pallas_call | solution.py:98
  12.8 0.9 %convert_element_type.12 = f16[2064,128]{1,0:T(8,128)(2,1)} convert(f32[2064,128]{1,0:T(8,128)S(1)} %get-tuple-element.33) | non-fusion elementwise | flops 264192 | bytes 1585152 | tf_op jit(solution)/shard_map/convert_element_type | solution.py:341
  13.7 0.9 %convert_element_type.13 = f16[2064,128]{1,0:T(8,128)(2,1)} convert(f32[2064,128]{1,0:T(8,128)S(1)} %get-tuple-element.34) | non-fusion elementwise | flops 264192 | bytes 1585152 | tf_op jit(solution)/shard_map/convert_element_type | solution.py:341
  14.6 2.0 %collective-permute-start.1 = (f16[2064,128]{1,0:T(8,128)(2,1)}, f16[2064,128]{1,0:T(8,128)(2,1)}, u32[]{:S(2)}, u32[]{:S(2)}) collective-permute-start(f16[2064,128]{1,0:T(8,128)(2,1)} %convert_element_type.13), channel_id=1, source_target_pairs={{0,1},{1,0},{2,3},{3,2},{4,5},{5,4},{6,7},{7,6},{8,9},{9,8},{10,11... | collective-permute-start | bytes 1585160 | tf_op jit(solution)/shard_map/ppermute | solution.py:342
  16.6 0.3 rev.11
  17.0 0.3 rev.10
  17.3 0.8 and_select_fusion
  18.1 0.3 rev.9
  18.5 1.0 %constant_dynamic-slice_fusion.own_ref = bf16[2048,256]{1,0:T(8,128)(2,1)} fusion(bf16[2048,512]{1,0:T(8,128)(2,1)S(1)} %bitcast.20, s32[]{:T(128)S(6)} %select_n.51), kind=kLoop, calls=%fused_computation.14 | loop fusion | bytes 2097156 | tf_op jit(solution)/shard_map/dynamic_slice | solution.py:343
  19.6 0.5 broadcast_in_dim.12.refs_3_
  20.0 10.8 %own_products.1 = (f32[2048,128]{1,0:T(8,128)S(1)}, f32[2048,128]{1,0:T(8,128)S(1)}, f32[2048,128]{1,0:T(8,128)S(1)}, f32[2048,128]{1,0:T(8,128)}) custom-call(s32[4]{0:T(128)S(1)} %pad_add_fusion.1.where_ref, bf16[2048,4096]{1,0:T(8,128)(2,1)} %bitcast.22, bf16[2048,256]{1,0:T(8,128)(2,1)} %constant_dynamic-slice_fusion.own_ref), custom_call_target="tpu_custom_call" | custom-call | flops 4294967296 | bytes 22020096 | tf_op jit(solution)/shard_map/own_products/pallas_call | solution.py:146
  30.9 1.0 %copy-done.1 = f32[2048,128]{1,0:T(8,128)} copy-done((f32[2048,128]{1,0:T(8,128)}, f32[2048,128]{1,0:T(8,128)S(1)}, u32[]{:S(2)}) %copy-start.1) | copy-done | bytes 1048600
  31.8 1.0 %copy-done.2 = f32[2048,128]{1,0:T(8,128)} copy-done((f32[2048,128]{1,0:T(8,128)}, f32[2048,128]{1,0:T(8,128)S(1)}, u32[]{:S(2)}) %copy-start.2) | copy-done | bytes 1048600
  32.8 8.4 %cross_product.1 = (f32[2048,128]{1,0:T(8,128)S(1)}, f32[2048,128]{1,0:T(8,128)S(1)}) custom-call(s32[4]{0:T(128)S(1)} %pad_add_fusion.1.where_ref, bf16[2048,4096]{1,0:T(8,128)(2,1)} %bitcast.23, bf16[2048,256]{1,0:T(8,128)(2,1)} %collective-permute-done.came_ref, f32[2048,128]{1,0:T(8,128)} %copy-done.1, f32[2048,128]{1,0:T(8,128)} %copy-done.2), custom_call_target="tpu_custom_call" | custom-call | flops 2147483648 | bytes 11534336 | tf_op jit(solution)/shard_map/cross_product/pallas_call | solution.py:98
  41.3 1.1 %convert_element_type.14.came_ref = f32[2064,128]{1,0:T(8,128)S(1)} convert(f16[2064,128]{1,0:T(8,128)(2,1)} %collective-permute-done.2) | non-fusion elementwise | flops 264192 | bytes 1585152 | tf_op jit(solution)/shard_map/convert_element_type | solution.py:355
  42.4 2.4 %settle.2 = (f32[4096,128]{1,0:T(8,128)S(1)}, bf16[1536,128]{1,0:T(8,128)(2,1)S(1)}) custom-call(s32[1536]{0:T(1024)S(1)} %get-tuple-element.38.list_ref, s32[1]{0:T(128)} %bitcast.5.live_ref, f32[2048,128]{1,0:T(8,128)S(1)} %get-tuple-element.44.here_ref, f32[2048,128]{1,0:T(8,128)S(1)} %get-tuple-element.45.far_ref, ...), custom_call_target="tpu_custom_call" | custom-call | bytes 5636096 | tf_op jit(solution)/shard_map/settle/pallas_call | solution.py:195
  44.8 3.2 %collective-permute-start.6 = (bf16[1536,128]{1,0:T(8,128)(2,1)S(1)}, bf16[1536,128]{1,0:T(8,128)(2,1)S(1)}, u32[]{:S(2)}, u32[]{:S(2)}) collective-permute-start(bf16[1536,128]{1,0:T(8,128)(2,1)S(1)} %get-tuple-element.47), channel_id=1, source_target_pairs={{0,30},{2,4},{4,2},{6,8},{8,6},{10,12},{12,10},{14,16},{16,14},{18... | collective-permute-start | bytes 1179656 | tf_op jit(solution)/shard_map/ppermute | solution.py:358
  48.0 2.1 %gather_rows.2 = bf16[1536,128]{1,0:T(8,128)(2,1)S(1)} custom-call(s32[1536]{0:T(1024)S(1)} %get-tuple-element.52.list_ref, f32[4096,128]{1,0:T(8,128)S(1)} %get-tuple-element.49.settled_ref.refs_4_), custom_call_target="tpu_custom_call" | custom-call | bytes 2490368 | tf_op jit(solution)/shard_map/gather_rows/pallas_call | solution.py:213
  50.1 0.1 collective-permute-start.5
  50.2 0.4 collective-permute-done.1
  50.6 1.1 %convert_element_type.15.came_ref = f32[2064,128]{1,0:T(8,128)S(1)} convert(f16[2064,128]{1,0:T(8,128)(2,1)} %collective-permute-done.1) | non-fusion elementwise | flops 264192 | bytes 1585152 | tf_op jit(solution)/shard_map/convert_element_type | solution.py:355
  51.7 2.4 %settle.3 = (f32[4096,128]{1,0:T(8,128)S(1)}, bf16[1536,128]{1,0:T(8,128)(2,1)S(1)}) custom-call(s32[1536]{0:T(1024)S(1)} %get-tuple-element.38.list_ref, s32[1]{0:T(128)} %bitcast.5.live_ref, f32[2048,128]{1,0:T(8,128)S(1)} %get-tuple-element.42.here_ref, f32[2048,128]{1,0:T(8,128)S(1)} %copy-done.3, f32[2064,128]{1,0:T(8,128)S(1)} %convert_element_type.15.came_ref), custom_call_target="tpu_custom_call" | custom-call | bytes 5636096 | tf_op jit(solution)/shard_map/settle/pallas_call | solution.py:195
  54.1 2.1 %gather_rows.3 = bf16[1536,128]{1,0:T(8,128)(2,1)S(1)} custom-call(s32[1536]{0:T(1024)S(1)} %get-tuple-element.52.list_ref, f32[4096,128]{1,0:T(8,128)S(1)} %get-tuple-element.53.settled_ref.refs_4_), custom_call_target="tpu_custom_call" | custom-call | bytes 2490368 | tf_op jit(solution)/shard_map/gather_rows/pallas_call | solution.py:213
  56.2 0.1 collective-permute-start.3
  56.4 4.8 %collective-permute-start.4 = (bf16[1536,128]{1,0:T(8,128)(2,1)S(1)}, bf16[1536,128]{1,0:T(8,128)(2,1)S(1)}, u32[]{:S(2)}, u32[]{:S(2)}) collective-permute-start(bf16[1536,128]{1,0:T(8,128)(2,1)S(1)} %get-tuple-element.51), channel_id=1, source_target_pairs={{0,30},{2,4},{4,2},{6,8},{8,6},{10,12},{12,10},{14,16},{16,14},{18... | collective-permute-start | bytes 1179656 | tf_op jit(solution)/shard_map/ppermute | solution.py:358
  61.2 0.1 pad_add_fusion.refs_0_
  61.3 7.5 %assemble.2.refs_7_ = f32[4096,256]{1,0:T(8,128)} custom-call(s32[2]{0:T(128)S(1)} %pad_add_fusion.refs_0_, s32[3072]{0:T(1024)S(1)} %reshape.12.refs_1_, s32[3072]{0:T(1024)S(1)} %reshape.13.refs_2_, f32[3072,128]{1,0:T(8,128)S(1)} %broadcast_in_dim.12.refs_3_, f32[4096,128]{1,0:T(8,128)S(1)} %get-tuple-element.49.settled_ref.refs_4_, ...), custom_call_target="tpu_custom_call" | custom-call | bytes 4980736 | tf_op jit(solution)/shard_map/assemble/pallas_call | solution.py:276
  68.9 7.5 %assemble.3 = f32[4096,256]{1,0:T(8,128)} custom-call(s32[2]{0:T(128)S(1)} %pad_add_fusion.refs_0_, s32[3072]{0:T(1024)S(1)} %reshape.12.refs_1_, s32[3072]{0:T(1024)S(1)} %reshape.13.refs_2_, f32[3072,128]{1,0:T(8,128)S(1)} %broadcast_in_dim.12.refs_3_, f32[4096,128]{1,0:T(8,128)S(1)} %get-tuple-element.53.settled_ref.refs_4_, ...), custom_call_target="tpu_custom_call", output_to_operand_aliasing={{}: (7, {})} | custom-call | bytes 4980736 | tf_op jit(solution)/shard_map/assemble/pallas_call | solution.py:276
  (25 shorter events, 0.2 us)
Async XLA Ops:
  0.0 1.6 %copy-start = (bf16[1,2048,512]{2,1,0:T(8,128)(2,1)S(1)}, bf16[1,2048,512]{2,1,0:T(8,128)(2,1)}, u32[]{:S(2)}) copy-start(bf16[1,2048,512]{2,1,0:T(8,128)(2,1)} %param.7) | copy-start | bytes 6291460
  1.7 31.2 %collective-permute-start = (bf16[2048,256]{1,0:T(8,128)(2,1)S(1)}, bf16[2048,256]{1,0:T(8,128)(2,1)}, u32[]{:S(2)}, u32[]{:S(2)}) collective-permute-start(bf16[2048,256]{1,0:T(8,128)(2,1)S(1)} %dynamic-slice_bitcast_fusion.other_ref), channel_id=1, source_target_pairs={{0,1},{1,0},{2,3},{3,2},{4,5},{5,4},{6,7},{7,6},{8,9},{9,8},{10,11... | collective-permute-start | bytes 3145736 | tf_op jit(solution)/shard_map/ppermute | solution.py:317
  12.8 3.8 %copy-start.4 = (f32[1,2,1536]{2,1,0:T(2,128)S(1)}, f32[1,2,1536]{2,1,0:T(2,128)}, u32[]{:S(2)}) copy-start(f32[1,2,1536]{2,1,0:T(2,128)} %param.13) | copy-start | bytes 36868
  12.8 4.1 %copy-start.5 = (s32[1,2,1536]{2,1,0:T(2,128)S(1)}, s32[1,2,1536]{2,1,0:T(2,128)}, u32[]{:S(2)}) copy-start(s32[1,2,1536]{2,1,0:T(2,128)} %param.12) | copy-start | bytes 36868
  12.8 4.5 %copy-start.6 = (s32[1,2,1536]{2,1,0:T(2,128)S(1)}, s32[1,2,1536]{2,1,0:T(2,128)}, u32[]{:S(2)}) copy-start(s32[1,2,1536]{2,1,0:T(2,128)} %param.11) | copy-start | bytes 36868
  13.7 27.5 %collective-permute-start.2 = (f16[2064,128]{1,0:T(8,128)(2,1)}, f16[2064,128]{1,0:T(8,128)(2,1)}, u32[]{:S(2)}, u32[]{:S(2)}) collective-permute-start(f16[2064,128]{1,0:T(8,128)(2,1)} %convert_element_type.12), channel_id=1, source_target_pairs={{0,1},{1,0},{2,3},{3,2},{4,5},{5,4},{6,7},{7,6},{8,9},{9,8},{10,11... | collective-permute-start | bytes 1585160 | tf_op jit(solution)/shard_map/ppermute | solution.py:342
  14.6 36.0 %collective-permute-start.1 = (f16[2064,128]{1,0:T(8,128)(2,1)}, f16[2064,128]{1,0:T(8,128)(2,1)}, u32[]{:S(2)}, u32[]{:S(2)}) collective-permute-start(f16[2064,128]{1,0:T(8,128)(2,1)} %convert_element_type.13), channel_id=1, source_target_pairs={{0,1},{1,0},{2,3},{3,2},{4,5},{5,4},{6,7},{7,6},{8,9},{9,8},{10,11... | collective-permute-start | bytes 1585160 | tf_op jit(solution)/shard_map/ppermute | solution.py:342
  30.9 1.0 %copy-start.1 = (f32[2048,128]{1,0:T(8,128)}, f32[2048,128]{1,0:T(8,128)S(1)}, u32[]{:S(2)}) copy-start(f32[2048,128]{1,0:T(8,128)S(1)} %get-tuple-element.40.rest_0_) | copy-start | bytes 3145732
  31.8 1.0 %copy-start.2 = (f32[2048,128]{1,0:T(8,128)}, f32[2048,128]{1,0:T(8,128)S(1)}, u32[]{:S(2)}) copy-start(f32[2048,128]{1,0:T(8,128)S(1)} %get-tuple-element.41.rest_1_) | copy-start | bytes 3145732
  44.8 7.0 %copy-start.3 = (f32[2048,128]{1,0:T(8,128)S(1)}, f32[2048,128]{1,0:T(8,128)}, u32[]{:S(2)}) copy-start(f32[2048,128]{1,0:T(8,128)} %get-tuple-element.43.far_ref) | copy-start | bytes 3145732
  44.8 16.5 %collective-permute-start.6 = (bf16[1536,128]{1,0:T(8,128)(2,1)S(1)}, bf16[1536,128]{1,0:T(8,128)(2,1)S(1)}, u32[]{:S(2)}, u32[]{:S(2)}) collective-permute-start(bf16[1536,128]{1,0:T(8,128)(2,1)S(1)} %get-tuple-element.47), channel_id=1, source_target_pairs={{0,30},{2,4},{4,2},{6,8},{8,6},{10,12},{12,10},{14,16},{16,14},{18... | collective-permute-start | bytes 1179656 | tf_op jit(solution)/shard_map/ppermute | solution.py:358
  50.1 11.2 %collective-permute-start.5 = (bf16[1536,128]{1,0:T(8,128)(2,1)S(1)}, bf16[1536,128]{1,0:T(8,128)(2,1)S(1)}, u32[]{:S(2)}, u32[]{:S(2)}) collective-permute-start(bf16[1536,128]{1,0:T(8,128)(2,1)S(1)} %gather_rows.2), channel_id=1, source_target_pairs={{0,2},{2,0},{4,6},{6,4},{8,10},{10,8},{12,14},{14,12},{16,18},{18,... | collective-permute-start | bytes 1179656 | tf_op jit(solution)/shard_map/ppermute | solution.py:360
  56.2 12.6 %collective-permute-start.3 = (bf16[1536,128]{1,0:T(8,128)(2,1)S(1)}, bf16[1536,128]{1,0:T(8,128)(2,1)S(1)}, u32[]{:S(2)}, u32[]{:S(2)}) collective-permute-start(bf16[1536,128]{1,0:T(8,128)(2,1)S(1)} %gather_rows.3), channel_id=1, source_target_pairs={{0,2},{2,0},{4,6},{6,4},{8,10},{10,8},{12,14},{14,12},{16,18},{18,... | collective-permute-start | bytes 1179656 | tf_op jit(solution)/shard_map/ppermute | solution.py:360
  56.4 12.5 %collective-permute-start.4 = (bf16[1536,128]{1,0:T(8,128)(2,1)S(1)}, bf16[1536,128]{1,0:T(8,128)(2,1)S(1)}, u32[]{:S(2)}, u32[]{:S(2)}) collective-permute-start(bf16[1536,128]{1,0:T(8,128)(2,1)S(1)} %get-tuple-element.51), channel_id=1, source_target_pairs={{0,30},{2,4},{4,2},{6,8},{8,6},{10,12},{12,10},{14,16},{16,14},{18... | collective-permute-start | bytes 1179656 | tf_op jit(solution)/shard_map/ppermute | solution.py:358

commit v3 on v2

--- a/solution.py
+++ b/solution.py
@@ -5,11 +5,13 @@
 from jax.experimental.pallas import tpu as pltpu
 from jax.sharding import PartitionSpec as P
 
+
 SMEM = pl.BlockSpec(memory_space=pltpu.SMEM)
 VMEM = pl.BlockSpec(memory_space=pltpu.VMEM)
 ANY = pl.BlockSpec(memory_space=pl.ANY)
 HBM = pl.BlockSpec(memory_space=pltpu.HBM)
 LANES = 128
+LIMIT = 50
 F32 = jnp.float32
 BF16 = jnp.bfloat16
 
@@ -76,22 +78,7 @@
         ref[pl.ds(rows, 16), :] = jnp.broadcast_to(power, (16, LANES))
 
 
-def cross_kernel(where_ref, flex_ref, came_ref, *rest):
-    count = (len(rest) - 2) // 2
-    nears, outs, buffer_ref, sems = rest[:count], rest[count:-2], rest[-2], rest[-1]
-    copies, tile = strips_of(flex_ref, where_ref[1], buffer_ref, sems)
-    right = masked(came_ref, where_ref[3])
-    for i, copy in enumerate(copies):
-        copy.wait()
-        span = pl.ds(i * tile, tile)
-        image = jnp.dot(buffer_ref[span, :], right, preferred_element_type=F32)
-        image = image + jnp.concatenate([ref[span, :] for ref in nears], axis=1)
-        ids = i * tile + lax.broadcasted_iota(jnp.int32, image.shape, 0)
-        image = jnp.where(ids < where_ref[2], image, jnp.zeros_like(image))
-        store_chunks(outs, span, image.astype(BF16).astype(F32))
-
-
-def product(kernel, name, out_shapes, where, flex, *rights):
+def product(kernel, out_shapes, where, flex, *rights):
     rows = flex.shape[0]
     width = rights[0].shape[1]
     strips = rows // tile_of(rows, 512)
@@ -104,68 +91,84 @@
             pltpu.VMEM((rows, rows), BF16),
             pltpu.SemaphoreType.DMA((strips,)),
         ],
-        compiler_params=params(50),
+        compiler_params=params(LIMIT),
         cost_estimate=cost(2 * rows * rows * width, 2 * rows * rows + 6 * rows * width),
-        name=name,
     )(where, flex, *rights)
 
 
-def own_kernel(where_ref, flex_ref, own_ref, *outs):
+def mirror_kernel(where_ref, flex_ref, own_ref, *outs):
+    right = masked(own_ref, where_ref[2])
+    far = lax.dot_general(
+        flex_ref[...], right, (((0,), (0,)), ((), ())), preferred_element_type=F32
+    )
+    store_chunks(outs, slice(None), far)
+
+
+def mirror_product(where, flex, own):
+    rows, width = own.shape
+    chunks = width // LANES
+    tile = tile_of(rows, 1024)
+    steps = rows // tile
+    return pl.pallas_call(
+        mirror_kernel,
+        out_shape=(jax.ShapeDtypeStruct((rows, LANES), F32),) * chunks,
+        grid_spec=pltpu.PrefetchScalarGridSpec(
+            num_scalar_prefetch=1,
+            grid=(steps,),
+            in_specs=[
+                pl.BlockSpec((rows, tile), lambda i, w: (0, w[1] * steps + i)),
+                pl.BlockSpec((rows, width), lambda i, w: (0, 0)),
+            ],
+            out_specs=(pl.BlockSpec((tile, LANES), lambda i, w: (i, 0)),) * chunks,
+        ),
+        compiler_params=params(LIMIT),
+        cost_estimate=cost(2 * rows * rows * width, 2 * rows * rows + 6 * rows * width),
+        name="mirror_product",
+    )(where, flex, own)
+
+
+def image_kernel(where_ref, flex_ref, own_ref, came_ref, *rest):
+    outs, whole_ref = rest[:-1], rest[-1]
+    rows = own_ref.shape[0]
     tile = flex_ref.shape[0]
-    rows = own_ref.shape[0]
-    chunks = len(outs) // 2
     step = pl.program_id(0)
-    right = masked(own_ref, where_ref[2])
-    columns = [pl.ds(pl.multiple_of(where_ref[b] * rows, rows), rows) for b in range(2)]
-    near = jnp.dot(flex_ref[:, columns[0]], right, preferred_element_type=F32)
-    store_chunks(outs[:chunks], slice(None), near)
-    span = pl.ds(pl.multiple_of(step * tile, tile), tile)
-    mine = own_ref[span, :]
-    ids = step * tile + lax.broadcasted_iota(jnp.int32, mine.shape, 0)
-    mine = jnp.where(ids < where_ref[2], mine, jnp.zeros_like(mine))
-    far = lax.dot_general(
-        flex_ref[:, columns[1]], mine, (((0,), (0,)), ((), ())), preferred_element_type=F32
-    )
-    for c, ref in enumerate(outs[chunks:]):
-        piece = far[:, c * LANES : (c + 1) * LANES]
-
-        @pl.when(step == 0)
-        def _():
-            ref[...] = piece
-
-        @pl.when(step > 0)
-        def _():
-            ref[...] = ref[...] + piece
-
-
-def own_products(where, flex, own):
+
+    @pl.when(step == 0)
+    def _():
+        for j, ref in enumerate((own_ref, came_ref)):
+            span = pl.ds(pl.multiple_of(where_ref[j] * rows, rows), rows)
+            whole_ref[span, :] = masked(ref, where_ref[2 + j])
+
+    image = jnp.dot(flex_ref[...], whole_ref[...], preferred_element_type=F32)
+    ids = step * tile + lax.broadcasted_iota(jnp.int32, image.shape, 0)
+    image = jnp.where(ids < where_ref[2], image, jnp.zeros_like(image))
+    store_chunks(outs, slice(None), image.astype(BF16).astype(F32))
+
+
+def image_product(where, flex, own, came):
     rows, width = own.shape
     chunks = width // LANES
     tile = tile_of(rows, 512)
-    shape = jax.ShapeDtypeStruct((rows, LANES), F32)
-    outs = pl.pallas_call(
-        own_kernel,
-        out_shape=(shape,) * (2 * chunks),
+    whole = pl.BlockSpec((rows, width), lambda i, w: (0, 0))
+    return pl.pallas_call(
+        image_kernel,
+        out_shape=(jax.ShapeDtypeStruct((rows, LANES), F32),) * chunks,
         grid_spec=pltpu.PrefetchScalarGridSpec(
             num_scalar_prefetch=1,
             grid=(rows // tile,),
-            in_specs=[
-                pl.BlockSpec((tile, 2 * rows), lambda i, w: (i, 0)),
-                pl.BlockSpec((rows, width), lambda i, w: (0, 0)),
-            ],
-            out_specs=(pl.BlockSpec((tile, LANES), lambda i, w: (i, 0)),) * chunks
-            + (pl.BlockSpec((rows, LANES), lambda i, w: (0, 0)),) * chunks,
+            in_specs=[pl.BlockSpec((tile, 2 * rows), lambda i, w: (i, 0)), whole, whole],
+            out_specs=(pl.BlockSpec((tile, LANES), lambda i, w: (i, 0)),) * chunks,
+            scratch_shapes=[pltpu.VMEM((2 * rows, width), BF16)],
         ),
-        compiler_params=params(50),
-        cost_estimate=cost(4 * rows * rows * width, 4 * rows * rows + 10 * rows * width),
-        name="own_products",
-    )(where, flex, own)
-    return outs[:chunks], outs[chunks:]
+        compiler_params=params(LIMIT),
+        cost_estimate=cost(4 * rows * rows * width, 4 * rows * rows + 6 * rows * width),
+        name="image_product",
+    )(where, flex, own, came)
 
 
 def pick_rows(list_ref, settled_ref, out_ref, rows_ref):
     count = out_ref.shape[0]
-    group = tile_of(count, 32)
+    group = tile_of(count, 128)
 
     def step(block, carry):
         first = pl.multiple_of(block * group, group)
@@ -222,42 +225,44 @@
     )(rows_list, settled)
 
 
-def assemble_kernel(
-    chunk, blocks_ref, targets_ref, places_ref, weights_ref, settled_ref, fast_ref, slow_ref, *rest
-):
-    out_ref, rows_refs, sums, sems = rest[-8], rest[-7:-5], rest[-5:-1], rest[-1]
-    rows_refs[0][...] = fast_ref[...].astype(F32)
-    rows_refs[1][...] = slow_ref[...].astype(F32)
-    for ref in sums:
-        ref[...] = jnp.zeros_like(ref)
-    count = fast_ref.shape[0]
-    group = tile_of(count, 32)
+def assemble_kernel(chunk, blocks_ref, *refs):
+    tables = (refs[0:3], refs[3:6])
+    settled_ref, cames = refs[6], refs[7:9]
+    out_ref, rows_refs, sums, sems = refs[-8], refs[-7:-5], refs[-5:-1], refs[-1]
+    for j in range(2):
+        rows_refs[j][...] = cames[j][...].astype(F32)
+        sums[2 * j + 1][...] = jnp.zeros_like(settled_ref)
+    sums[0][...] = settled_ref[...]
+    sums[2][...] = jnp.zeros_like(settled_ref)
+    count = cames[0].shape[0]
+    group = tile_of(count, 64)
 
     def step(block, carry):
         start = pl.multiple_of(block * group, group)
         for k in range(group):
+            s = start + k
             for j in range(2):
-                s = j * count + start + k
+                targets_ref, places_ref, weights_ref = tables[j]
                 row = targets_ref[s]
                 at = places_ref[s]
                 weight = weights_ref[pl.ds(s, 1), :]
                 first = rows_refs[j][pl.ds(at, 1), :]
                 second = rows_refs[j][pl.ds(at + 1, 1), :]
                 jump = (1.0 - weight) * first + weight * second
-                total = sums[(k % 2) * 2 + j]
-                total[pl.ds(row, 1), :] = total[pl.ds(row, 1), :] + jump
+                total = sums[2 * (k % 2) + j]
+                total[pl.ds(row, 1), :] = total[pl.ds(row, 1), :] - jump
         return carry
 
     lax.fori_loop(0, count // group, step, 0)
     rows = settled_ref.shape[0]
-    piece = rows // 4
+    piece = rows // 8
     copies = []
-    for q in range(4):
+    for q in range(8):
         span = pl.ds(q * piece, piece)
-        sums[0][span, :] = settled_ref[span, :] - (
-            (sums[0][span, :] + sums[1][span, :]) + (sums[2][span, :] + sums[3][span, :])
+        sums[0][span, :] = (sums[0][span, :] + sums[1][span, :]) + (
+            sums[2][span, :] + sums[3][span, :]
         )
-        target = pl.multiple_of(blocks_ref[q // 2] * (rows // 2) + (q % 2) * piece, piece)
+        target = pl.multiple_of(blocks_ref[q // 4] * (rows // 2) + (q % 4) * piece, piece)
         copy = pltpu.make_async_copy(
             sums[0].at[span, :],
             out_ref.at[pl.ds(target, piece), pl.ds(chunk * LANES, LANES)],
@@ -269,23 +274,23 @@
         copy.wait()
 
 
-def assemble(chunk, width, blocks, targets, places, weights, settled, fast, slow, before):
+def assemble(chunk, width, blocks, tables, settled, fast, slow, before):
     rows = settled.shape[0]
     count = fast.shape[0]
     more = [] if before is None else [before]
     return pl.pallas_call(
         lambda *refs: assemble_kernel(chunk, *refs),
         out_shape=jax.ShapeDtypeStruct((rows, width), F32),
-        in_specs=[SMEM, SMEM, SMEM, VMEM, VMEM, VMEM, VMEM] + [ANY] * len(more),
+        in_specs=[SMEM] + [SMEM, SMEM, VMEM] * 2 + [VMEM] * 3 + [ANY] * len(more),
         out_specs=ANY,
         scratch_shapes=[pltpu.VMEM((count, LANES), F32)] * 2
         + [pltpu.VMEM((rows, LANES), F32)] * 4
-        + [pltpu.SemaphoreType.DMA((4,))],
-        input_output_aliases={7: 0} if more else {},
+        + [pltpu.SemaphoreType.DMA((8,))],
+        input_output_aliases={10: 0} if more else {},
         compiler_params=params(20),
         cost_estimate=cost(0, 8 * settled.size + 4 * fast.size),
         name="assemble",
-    )(blocks, targets, places, weights, settled, fast, slow, *more)
+    )(blocks, *tables[0], *tables[1], settled, fast, slow, *more)
 
 
 def after(value, *earlier):
@@ -315,7 +320,6 @@
     where = jnp.stack([me, other, live_here, live_there]).astype(jnp.int32)
     others = lax.dynamic_slice_in_dim(block, other * width, width, axis=1)
     came = lax.ppermute(others, "panel", swap)
-    strip = (rows, LANES)
 
     def local_order(index):
         return (index + me * rows) % (2 * rows)
@@ -323,47 +327,41 @@
     lists = local_order(send_rows[region])
     slow_list, fast_list = lists[side], lists[1 - side]
 
-    def ordered(table):
-        return jnp.where(side == 0, table[::-1], table).reshape(-1)
-
-    targets = ordered(local_order(recv_rows[0]))
-    places = ordered(recv_pos[0])
-    weights = jnp.broadcast_to(ordered(recv_weight[0])[:, None], (targets.shape[0], LANES))
+    recv_local = local_order(recv_rows[0])
+    tables = []
+    for j in (1 - side, side):
+        weight = jnp.broadcast_to(recv_weight[0][j][:, None], (recv_rows.shape[2], LANES))
+        tables.append((recv_local[j], recv_pos[0][j], weight))
     blocks = where[:2]
     live = live_there[None]
 
-    parts = product(
-        part_kernel, "part_product", [(rows + 16, LANES)] * chunks, where, flex, others
+    own = lax.dynamic_slice_in_dim(after(block, others), me * width, width, axis=1)
+    own, tables, slow_list, fast_list, blocks, live, held = lax.optimization_barrier(
+        (own, tables, slow_list, fast_list, blocks, live, others)
     )
+    parts = product(part_kernel, [(rows + 16, LANES)] * chunks, where, flex, held)
     payloads = []
     order = others
     for c in range(chunks):
         order = after(parts[c], order).astype(jnp.float16)
         payloads.append(lax.ppermute(order, "panel", swap))
-    own = lax.dynamic_slice_in_dim(after(block, order), me * width, width, axis=1)
-    own, targets, places, weights, slow_list, fast_list = lax.optimization_barrier(
-        (own, targets, places, weights, slow_list, fast_list)
-    )
-    nears, fars = own_products(where, flex, own)
-    heres = product(
-        cross_kernel, "cross_product", [strip] * chunks, where, flex, came, *nears
-    )
+    fars = mirror_product(where, flex, after(own, order))
+    own = after(own, fars)
+    heres = image_product(where, flex, own, came)
 
     settled, slow, fast = [], [], []
     last = heres[0]
     for c in range(chunks):
         arrived = after(payloads[c], last).astype(F32)
         whole, sent = settle(slow_list, live, heres[c], fars[c], arrived)
-        settled.append(whole)
         slow.append(lax.ppermute(sent, "region", outer))
         last = gather_rows(after(fast_list, sent), whole)
         fast.append(lax.ppermute(last, "region", inner))
-    targets = after(targets, last)
+        settled.append(whole)
+    blocks = after(blocks, last)
     result = None
     for c in range(chunks):
-        result = assemble(
-            c, width, blocks, targets, places, weights, settled[c], fast[c], slow[c], result
-        )
+        result = assemble(c, width, blocks, tables, settled[c], fast[c], slow[c], result)
     return result[None]
 
 

time: 76.9 us -> 74.5 us (0.969)
  waiting for transfers between devices: 0.44 us -> 11.5 us
  Pallas kernels: 50.7 us -> 45.4 us
  local copies, waits for them, and re-layouts: 6.14 us -> 2.41 us
  other arithmetic: 4.91 us -> 1.19 us
    pallas_call x2 -> x1, Pallas kernels: 15.8 us -> 7.37 us  [product(): pl.pallas_call(kernel, out_shape=tuple((jax.ShapeDtypeStruct(shape, F32)...]
    ppermute x1, waiting for transfers between devices: 0.01 us -> 6.49 us  [on_device(): came = lax.ppermute(others, 'panel', swap)]
    ppermute x2, waiting for transfers between devices: 0.43 us -> 5.04 us  [on_device(): payloads.append(lax.ppermute(order, 'panel', swap))]
    pallas_call x1 -> x2, Pallas kernels: 10.8 us -> 15.2 us  [the longest x1 9.69 us: image_product(): pl.pallas_call(image_kernel, out_shape=(jax.ShapeDtypeStruct((rows, LANES...]
    convert_element_type x2, other arithmetic: 2.23 us -> 0.14 us  [on_device(): arrived = after(payloads[c], last).astype(F32)]
    unnamed x14 -> x8, local copies, waits for them, and re-layouts: 3.55 us -> 1.59 us
    convert_element_type x2, other arithmetic: 1.75 us -> 0.14 us  [on_device(): order = after(parts[c], order).astype(jnp.float16)]
    rev x3 -> x0, local copies, waits for them, and re-layouts: 0.93 us -> none  [ordered(): return jnp.where(side == 0, table[::-1], table).reshape(-1)]
  transfers between devices with their start and end apart: 7 -> 7, of which waited for: 1 -> 3; matrix products, arithmetic and copies ran while one was open for 10% -> 3% of each run, Pallas kernels for 56% -> 51%
where the time goes in v3:
time: 74.5 us; the launch traced here: 74.3 us
  Pallas kernels  45.4 us (61%)
  starting transfers between devices  12.8 us (17%)
  waiting for transfers between devices  11.5 us (15%)
  local copies, waits for them, and re-layouts  2.41 us (3%)
  other arithmetic  1.19 us (2%)
  between operations  0.88 us (1%)
    pallas_call x2, Pallas kernels, assemble(): pl.pallas_call(lambda *refs: assemble_kernel(chunk, *refs), out_shape=jax...  14.5 us
    pallas_call x1, Pallas kernels, image_product(): pl.pallas_call(image_kernel, out_shape=(jax.ShapeDtypeStruct((rows, LANES...  9.69 us
    ppermute x2, starting transfers between devices, on_device(): slow.append(lax.ppermute(sent, 'region', outer))  7.51 us
    pallas_call x1, Pallas kernels, product(): pl.pallas_call(kernel, out_shape=tuple((jax.ShapeDtypeStruct(shape, F32)...  7.37 us
    ppermute x1, waiting for transfers between devices, on_device(): came = lax.ppermute(others, 'panel', swap)  6.49 us
    pallas_call x1, Pallas kernels, mirror_product(): pl.pallas_call(mirror_kernel, out_shape=(jax.ShapeDtypeStruct((rows, LANE...  5.51 us
    ppermute x2, waiting for transfers between devices, on_device(): payloads.append(lax.ppermute(order, 'panel', swap))  5.04 us
    pallas_call x2, Pallas kernels, settle(): pl.pallas_call(settle_kernel, out_shape=(jax.ShapeDtypeStruct((2 * rows,...  4.47 us
  transfers between devices with their start and end apart: 7, of which 3 were waited for; matrix products, arithmetic and copies ran while one was open for 3% of the time, Pallas kernels for 51%

profile of v3, /device:TPU:0, one launch (start us, length us, event | category | flops | bytes accessed | tf_op | source)
XLA Modules:
  0.0 74.3 jit_solution(3557513891348818999)
XLA Ops:
  0.0 1.6 %copy-done = bf16[1,2048,512]{2,1,0:T(8,128)(2,1)S(1)} copy-done((bf16[1,2048,512]{2,1,0:T(8,128)(2,1)S(1)}, bf16[1,2048,512]{2,1,0:T(8,128)(2,1)}, u32[]{:S(2)}) %copy-start) | copy-done | bytes 2097176
  1.6 0.1 dynamic-slice_bitcast_fusion.other_ref
  1.7 3.0 %collective-permute-start = (bf16[2048,256]{1,0:T(8,128)(2,1)S(1)}, bf16[2048,256]{1,0:T(8,128)(2,1)}, u32[]{:S(2)}, u32[]{:S(2)}) collective-permute-start(bf16[2048,256]{1,0:T(8,128)(2,1)S(1)} %dynamic-slice_bitcast_fusion.other_ref), channel_id=1, source_target_pairs={{0,1},{1,0},{2,3},{3,2},{4,5},{5,4},{6,7},{7,6},{8,9},{9,8},{10,11... | collective-permute-start | bytes 3145736 | tf_op jit(solution)/shard_map/ppermute | solution.py:322
  4.7 0.7 %and_select_fusion = (s32[2,1536]{1,0:T(2,128)S(1)}, s32[2,1536]{1,0:T(2,128)S(1)}) fusion(s32[16,2,1536]{2,1,0:T(2,128)} %param.10, s32[]{:T(128)S(6)} %select_n.44, s32[]{:T(128)S(6)} %mul.16, s32[1,2,1536]{2,1,0:T(2,128)S(1)} %copy-done.1), kind=kLoop, calls=%fused_computation.5 | loop fusion | flops 73728 | bytes 49160 | tf_op jit(solution)/shard_map/jit(remainder)/select_n | solution.py:325
  6.3 0.1 pad_add_fusion.refs_0_
  6.4 0.1 constant_dynamic-slice_fusion.own_ref
  6.5 0.3 broadcast_in_dim.21.refs_6_
  6.8 0.3 broadcast_in_dim.19.refs_3_
  7.0 0.1 pad_add_fusion.1.where_ref
  7.1 7.4 %shard_map.73 = (f32[2064,128]{1,0:T(8,128)S(1)}, f32[2064,128]{1,0:T(8,128)S(1)}) custom-call(s32[4]{0:T(128)S(1)} %pad_add_fusion.1.where_ref, bf16[2048,4096]{1,0:T(8,128)(2,1)} %bitcast.17, bf16[2048,256]{1,0:T(8,128)(2,1)S(1)} %dynamic-slice_bitcast_fusion.other_ref), custom_call_target="tpu_custom_call" | custom-call | flops 2147483648 | bytes 11534336 | tf_op jit(solution)/shard_map/pallas_call | solution.py:85
  14.5 0.1 convert_element_type.12
  14.6 0.1 collective-permute-start.2
  14.7 0.1 convert_element_type.13
  14.7 2.1 %collective-permute-start.1 = (f16[2064,128]{1,0:T(8,128)(2,1)S(1)}, f16[2064,128]{1,0:T(8,128)(2,1)S(1)}, u32[]{:S(2)}, u32[]{:S(2)}) collective-permute-start(f16[2064,128]{1,0:T(8,128)(2,1)S(1)} %convert_element_type.13), channel_id=1, source_target_pairs={{0,1},{1,0},{2,3},{3,2},{4,5},{5,4},{6,7},{7,6},{8,9},{9,8},{10,11... | collective-permute-start | bytes 1585160 | tf_op jit(solution)/shard_map/ppermute | solution.py:347
  16.8 5.5 %mirror_product.1 = (f32[2048,128]{1,0:T(8,128)S(1)}, f32[2048,128]{1,0:T(8,128)S(1)}) custom-call(s32[4]{0:T(128)S(1)} %pad_add_fusion.1.where_ref, bf16[2048,4096]{1,0:T(8,128)(2,1)} %bitcast.18, bf16[2048,256]{1,0:T(8,128)(2,1)S(1)} %constant_dynamic-slice_fusion.own_ref), custom_call_target="tpu_custom_call" | custom-call | flops 2147483648 | bytes 11534336 | tf_op jit(solution)/shard_map/mirror_product/pallas_call | solution.py:112
  22.3 6.5 %collective-permute-done.came_ref = bf16[2048,256]{1,0:T(8,128)(2,1)} collective-permute-done((bf16[2048,256]{1,0:T(8,128)(2,1)S(1)}, bf16[2048,256]{1,0:T(8,128)(2,1)}, u32[]{:S(2)}, u32[]{:S(2)}) %collective-permute-start) | collective-permute-done | bytes 1048608 | tf_op jit(solution)/shard_map/ppermute | solution.py:322
  28.8 9.7 %image_product.1 = (f32[2048,128]{1,0:T(8,128)S(1)}, f32[2048,128]{1,0:T(8,128)S(1)}) custom-call(s32[4]{0:T(128)S(1)} %pad_add_fusion.1.where_ref, bf16[2048,4096]{1,0:T(8,128)(2,1)} %bitcast.19, bf16[2048,256]{1,0:T(8,128)(2,1)S(1)} %constant_dynamic-slice_fusion.own_ref, bf16[2048,256]{1,0:T(8,128)(2,1)} %collective-permute-done.came_ref), custom_call_target="tpu_custom_call" | custom-call | flops 4294967296 | bytes 19922944 | tf_op jit(solution)/shard_map/image_product/pallas_call | solution.py:153
  38.5 1.5 %collective-permute-done.2 = f16[2064,128]{1,0:T(8,128)(2,1)S(1)} collective-permute-done((f16[2064,128]{1,0:T(8,128)(2,1)S(1)}, f16[2064,128]{1,0:T(8,128)(2,1)S(1)}, u32[]{:S(2)}, u32[]{:S(2)}) %collective-permute-start.2) | collective-permute-done | bytes 528416 | tf_op jit(solution)/shard_map/ppermute | solution.py:347
  40.0 0.1 convert_element_type.14.came_ref
  40.1 2.2 %settle.2 = (f32[4096,128]{1,0:T(8,128)S(1)}, bf16[1536,128]{1,0:T(8,128)(2,1)S(1)}) custom-call(s32[1536]{0:T(1024)S(1)} %get-tuple-element.40.list_ref, s32[1]{0:T(128)} %bitcast.7.live_ref, f32[2048,128]{1,0:T(8,128)S(1)} %get-tuple-element.53.here_ref, f32[2048,128]{1,0:T(8,128)S(1)} %get-tuple-element.49.far_ref, ...), custom_call_target="tpu_custom_call" | custom-call | bytes 5636096 | tf_op jit(solution)/shard_map/settle/pallas_call | solution.py:198
  42.3 2.6 %collective-permute-start.6 = (bf16[1536,128]{1,0:T(8,128)(2,1)S(1)}, bf16[1536,128]{1,0:T(8,128)(2,1)S(1)}, u32[]{:S(2)}, u32[]{:S(2)}) collective-permute-start(bf16[1536,128]{1,0:T(8,128)(2,1)S(1)} %get-tuple-element.55), channel_id=1, source_target_pairs={{0,30},{2,4},{4,2},{6,8},{8,6},{10,12},{12,10},{14,16},{16,14},{18... | collective-permute-start | bytes 1179656 | tf_op jit(solution)/shard_map/ppermute | solution.py:357
  45.0 1.9 %gather_rows.2 = bf16[1536,128]{1,0:T(8,128)(2,1)S(1)} custom-call(s32[1536]{0:T(1024)S(1)} %get-tuple-element.60.list_ref, f32[4096,128]{1,0:T(8,128)S(1)} %get-tuple-element.57.settled_ref.refs_7_), custom_call_target="tpu_custom_call" | custom-call | bytes 2490368 | tf_op jit(solution)/shard_map/gather_rows/pallas_call | solution.py:216
  46.9 0.1 collective-permute-start.5
  47.0 3.5 %collective-permute-done.1 = f16[2064,128]{1,0:T(8,128)(2,1)S(1)} collective-permute-done((f16[2064,128]{1,0:T(8,128)(2,1)S(1)}, f16[2064,128]{1,0:T(8,128)(2,1)S(1)}, u32[]{:S(2)}, u32[]{:S(2)}) %collective-permute-start.1) | collective-permute-done | bytes 528416 | tf_op jit(solution)/shard_map/ppermute | solution.py:347
  50.5 0.1 convert_element_type.15.came_ref
  50.6 2.2 %settle.3 = (f32[4096,128]{1,0:T(8,128)S(1)}, bf16[1536,128]{1,0:T(8,128)(2,1)S(1)}) custom-call(s32[1536]{0:T(1024)S(1)} %get-tuple-element.40.list_ref, s32[1]{0:T(128)} %bitcast.7.live_ref, f32[2048,128]{1,0:T(8,128)S(1)} %get-tuple-element.52.here_ref, f32[2048,128]{1,0:T(8,128)S(1)} %get-tuple-element.50.far_ref, ...), custom_call_target="tpu_custom_call" | custom-call | bytes 5636096 | tf_op jit(solution)/shard_map/settle/pallas_call | solution.py:198
  52.8 1.9 %gather_rows.3 = bf16[1536,128]{1,0:T(8,128)(2,1)S(1)} custom-call(s32[1536]{0:T(1024)S(1)} %get-tuple-element.60.list_ref, f32[4096,128]{1,0:T(8,128)S(1)} %get-tuple-element.61.settled_ref.refs_7_), custom_call_target="tpu_custom_call" | custom-call | bytes 2490368 | tf_op jit(solution)/shard_map/gather_rows/pallas_call | solution.py:216
  54.8 0.1 collective-permute-start.3
  54.8 4.9 %collective-permute-start.4 = (bf16[1536,128]{1,0:T(8,128)(2,1)S(1)}, bf16[1536,128]{1,0:T(8,128)(2,1)S(1)}, u32[]{:S(2)}, u32[]{:S(2)}) collective-permute-start(bf16[1536,128]{1,0:T(8,128)(2,1)S(1)} %get-tuple-element.59), channel_id=1, source_target_pairs={{0,30},{2,4},{4,2},{6,8},{8,6},{10,12},{12,10},{14,16},{16,14},{18... | collective-permute-start | bytes 1179656 | tf_op jit(solution)/shard_map/ppermute | solution.py:357
  59.8 7.2 %assemble.2.refs_10_ = f32[4096,256]{1,0:T(8,128)} custom-call(s32[2]{0:T(128)S(1)} %pad_add_fusion.refs_0_, s32[1536]{0:T(1024)S(1)} %get-tuple-element.63.refs_1_, s32[1536]{0:T(1024)S(1)} %get-tuple-element.64.refs_2_, f32[1536,128]{1,0:T(8,128)S(1)} %broadcast_in_dim.19.refs_3_, s32[1536]{0:T(1024)S(1)} %get-tuple-element.66.refs_4_, ...), custom_call_target="tpu_custom_call" | custom-call | bytes 4980736 | tf_op jit(solution)/shard_map/assemble/pallas_call | solution.py:281
  67.0 0.0 collective-permute-done.3.refs_8_
  67.0 7.2 %assemble.3 = f32[4096,256]{1,0:T(8,128)} custom-call(s32[2]{0:T(128)S(1)} %pad_add_fusion.refs_0_, s32[1536]{0:T(1024)S(1)} %get-tuple-element.63.refs_1_, s32[1536]{0:T(1024)S(1)} %get-tuple-element.64.refs_2_, f32[1536,128]{1,0:T(8,128)S(1)} %broadcast_in_dim.19.refs_3_, s32[1536]{0:T(1024)S(1)} %get-tuple-element.66.refs_4_, ...), custom_call_target="tpu_custom_call", output_to_operand_aliasing={{}: (10, {})} | custom-call | bytes 4980736 | tf_op jit(solution)/shard_map/assemble/pallas_call | solution.py:281
  (14 shorter events, 0.2 us)
Async XLA Ops:
  0.0 1.6 %copy-start = (bf16[1,2048,512]{2,1,0:T(8,128)(2,1)S(1)}, bf16[1,2048,512]{2,1,0:T(8,128)(2,1)}, u32[]{:S(2)}) copy-start(bf16[1,2048,512]{2,1,0:T(8,128)(2,1)} %param.7) | copy-start | bytes 6291460
  0.0 4.7 %copy-start.1 = (s32[1,2,1536]{2,1,0:T(2,128)S(1)}, s32[1,2,1536]{2,1,0:T(2,128)}, u32[]{:S(2)}) copy-start(s32[1,2,1536]{2,1,0:T(2,128)} %param.11) | copy-start | bytes 36868
  0.0 6.1 %copy-start.2 = (s32[1,2,1536]{2,1,0:T(2,128)S(1)}, s32[1,2,1536]{2,1,0:T(2,128)}, u32[]{:S(2)}) copy-start(s32[1,2,1536]{2,1,0:T(2,128)} %param.12) | copy-start | bytes 36868
  0.0 6.2 %copy-start.3 = (f32[1,2,1536]{2,1,0:T(2,128)S(1)}, f32[1,2,1536]{2,1,0:T(2,128)}, u32[]{:S(2)}) copy-start(f32[1,2,1536]{2,1,0:T(2,128)} %param.13) | copy-start | bytes 36868
  1.7 27.1 %collective-permute-start = (bf16[2048,256]{1,0:T(8,128)(2,1)S(1)}, bf16[2048,256]{1,0:T(8,128)(2,1)}, u32[]{:S(2)}, u32[]{:S(2)}) collective-permute-start(bf16[2048,256]{1,0:T(8,128)(2,1)S(1)} %dynamic-slice_bitcast_fusion.other_ref), channel_id=1, source_target_pairs={{0,1},{1,0},{2,3},{3,2},{4,5},{5,4},{6,7},{7,6},{8,9},{9,8},{10,11... | collective-permute-start | bytes 3145736 | tf_op jit(solution)/shard_map/ppermute | solution.py:322
  14.6 25.5 %collective-permute-start.2 = (f16[2064,128]{1,0:T(8,128)(2,1)S(1)}, f16[2064,128]{1,0:T(8,128)(2,1)S(1)}, u32[]{:S(2)}, u32[]{:S(2)}) collective-permute-start(f16[2064,128]{1,0:T(8,128)(2,1)S(1)} %convert_element_type.12), channel_id=1, source_target_pairs={{0,1},{1,0},{2,3},{3,2},{4,5},{5,4},{6,7},{7,6},{8,9},{9,8},{10,11... | collective-permute-start | bytes 1585160 | tf_op jit(solution)/shard_map/ppermute | solution.py:347
  14.7 35.8 %collective-permute-start.1 = (f16[2064,128]{1,0:T(8,128)(2,1)S(1)}, f16[2064,128]{1,0:T(8,128)(2,1)S(1)}, u32[]{:S(2)}, u32[]{:S(2)}) collective-permute-start(f16[2064,128]{1,0:T(8,128)(2,1)S(1)} %convert_element_type.13), channel_id=1, source_target_pairs={{0,1},{1,0},{2,3},{3,2},{4,5},{5,4},{6,7},{7,6},{8,9},{9,8},{10,11... | collective-permute-start | bytes 1585160 | tf_op jit(solution)/shard_map/ppermute | solution.py:347
  42.3 17.4 %collective-permute-start.6 = (bf16[1536,128]{1,0:T(8,128)(2,1)S(1)}, bf16[1536,128]{1,0:T(8,128)(2,1)S(1)}, u32[]{:S(2)}, u32[]{:S(2)}) collective-permute-start(bf16[1536,128]{1,0:T(8,128)(2,1)S(1)} %get-tuple-element.55), channel_id=1, source_target_pairs={{0,30},{2,4},{4,2},{6,8},{8,6},{10,12},{12,10},{14,16},{16,14},{18... | collective-permute-start | bytes 1179656 | tf_op jit(solution)/shard_map/ppermute | solution.py:357
  46.9 12.9 %collective-permute-start.5 = (bf16[1536,128]{1,0:T(8,128)(2,1)S(1)}, bf16[1536,128]{1,0:T(8,128)(2,1)S(1)}, u32[]{:S(2)}, u32[]{:S(2)}) collective-permute-start(bf16[1536,128]{1,0:T(8,128)(2,1)S(1)} %gather_rows.2), channel_id=1, source_target_pairs={{0,2},{2,0},{4,6},{6,4},{8,10},{10,8},{12,14},{14,12},{16,18},{18,... | collective-permute-start | bytes 1179656 | tf_op jit(solution)/shard_map/ppermute | solution.py:359
  54.8 12.2 %collective-permute-start.3 = (bf16[1536,128]{1,0:T(8,128)(2,1)S(1)}, bf16[1536,128]{1,0:T(8,128)(2,1)S(1)}, u32[]{:S(2)}, u32[]{:S(2)}) collective-permute-start(bf16[1536,128]{1,0:T(8,128)(2,1)S(1)} %gather_rows.3), channel_id=1, source_target_pairs={{0,2},{2,0},{4,6},{6,4},{8,10},{10,8},{12,14},{14,12},{16,18},{18,... | collective-permute-start | bytes 1179656 | tf_op jit(solution)/shard_map/ppermute | solution.py:359
  54.8 12.2 %collective-permute-start.4 = (bf16[1536,128]{1,0:T(8,128)(2,1)S(1)}, bf16[1536,128]{1,0:T(8,128)(2,1)S(1)}, u32[]{:S(2)}, u32[]{:S(2)}) collective-permute-start(bf16[1536,128]{1,0:T(8,128)(2,1)S(1)} %get-tuple-element.59), channel_id=1, source_target_pairs={{0,30},{2,4},{4,2},{6,8},{8,6},{10,12},{12,10},{14,16},{16,14},{18... | collective-permute-start | bytes 1179656 | tf_op jit(solution)/shard_map/ppermute | solution.py:357
